TPU v7x, 128 devices: a whole 4x4x4 slice. The times are simulated.
128 devices in a mesh: trial: 2 (over core), tmpl: 64 (over z, x, y).
Axes of the slice: x: 4, y: 4, z: 4, core: 2. Of those that a mesh axis runs over, the one named last changes fastest.
Arguments:
- spectra: bfloat16 [2, 2, 64, 2, 16896], P(None, 'trial', 'tmpl'), may hold values from -6 to 6
- half_spectra: bfloat16 [2, 2, 64, 2, 8704], P(None, 'trial', 'tmpl'), may hold values from -6 to 6
- kernels: bfloat16 [1024, 2, 512], P('tmpl'), may hold values from -0.1875 to 0.1875
- owners: int32 [2, 2], replicated, may hold values from 0 to 127, as said below
- counts: int32 [64], replicated, may hold values from 12 to 16, as said below
- partners: int32 [1024], replicated, may hold values from -1 to 1023, as said below
Outputs:
- powers: bfloat16 [2, 2, 1024, 16384], P(None, 'trial', 'tmpl')
Inputs may be any that keep to these rules, and one draw needn't show every extreme that they name: owners[w, t] = i * 64 + c names the device with trial index i and tmpl index c that holds window w's data of trial t; the two trials of a window lie on different trial indices, and the trial index holding trial 0 alternates from one window to the next; in some window the two trials lie on devices 0 and 127. The live templates of tmpl index d are its first counts[d]; some index has all 16 live. For a live template j, partners[j] is a live template; the live templates of one tmpl index name templates of any one tmpl index at most 1 times, and some index does so exactly 1 times; partners[j] = -1 for every template that is not live.
All inputs are finite; a program needn't handle non-finite values.
Results may differ from a plain program's by a relative error of at most 0.004.
Values may be sent and summed in bfloat16 or wider, within the bound.
No kernel may reach another device: no remote copies, remote signals or barrier semaphores. Data moves between devices by JAX's collectives and lax.ppermute only.
A program may use at most 128 MiB of HBM per device.

v0:
```python
import jax
import jax.numpy as jnp
from jax import lax
from jax.sharding import Mesh
from jax.sharding import PartitionSpec as P

TMPL = ("tmpl_0", "tmpl_1", "tmpl_2")


def spread(x, axes, root):
    x = jnp.where(lax.axis_index(axes) == root, x, jnp.zeros_like(x))
    for axis in axes:
        x = lax.psum(x, axis)
    return x


def swapped(x, axis, bit):
    return lax.ppermute(x, axis, [(i, i ^ 1 << bit) for i in range(lax.axis_size(axis))])


def hankel_rows(signal, tap_count, columns):
    length = signal.shape[1]
    repeated = jnp.broadcast_to(signal[:, None, :], (2, tap_count + 1, length)).reshape(
        2, (tap_count + 1) * length
    )
    skewed = repeated[:, : tap_count * (length + 1)].reshape(2, tap_count, length + 1)
    return skewed[:, :, :columns].reshape(2 * tap_count, columns)


def kernel_matrix(kernel_set):
    real_part = kernel_set[:, 0, :]
    imag_part = kernel_set[:, 1, :]
    upper_rows = jnp.concatenate([real_part, -imag_part], axis=1)
    lower_rows = jnp.concatenate([imag_part, real_part], axis=1)
    return jnp.concatenate([upper_rows, lower_rows], axis=0)


def power_rows(weights, stacked):
    product = jnp.dot(weights, stacked, preferred_element_type=jnp.float32)
    middle = weights.shape[0] // 2
    return product[:middle] * product[:middle] + product[middle:] * product[middle:]


def blocked_powers(weights, signal, tap_count, columns):
    block_rows = min(columns, 1024)

    def add_block(number, result):
        first_bin = number * block_rows
        segment = lax.dynamic_slice_in_dim(signal, first_bin, block_rows + tap_count, 1)
        values = power_rows(weights, hankel_rows(segment, tap_count, block_rows))
        return lax.dynamic_update_slice_in_dim(result, values, first_bin, 1)

    initial = jnp.zeros((weights.shape[0] // 2, columns), jnp.float32)
    return lax.fori_loop(0, columns // block_rows, add_block, initial)


def read_plan(partners, counts, per_device, width):
    pair_table = partners.reshape(width, per_device)
    positions = jnp.arange(per_device, dtype=jnp.int32)
    live_mask = positions[None, :] < counts[:, None]
    source = jnp.where(live_mask, pair_table // per_device, -1)
    holder_slot = pair_table % per_device
    earlier = positions[:, None] > positions[None, :]
    matches = (source[:, :, None] == source[:, None, :]) & earlier[None, :, :]
    ranking = jnp.sum(matches.astype(jnp.int32), axis=2)
    return (live_mask, source, holder_slot, ranking)


def body(spectra, half_spectra, kernels, owners, counts, partners):
    width = lax.axis_size(TMPL)
    device = lax.axis_index(TMPL)
    trial_index = lax.axis_index("trial")
    per_device = kernels.shape[0]
    tap_count = kernels.shape[2]
    windows = spectra.shape[0]
    bins_whole = spectra.shape[4] - tap_count
    bins_half = half_spectra.shape[4] - tap_count
    capacity = max(1, per_device // width)
    weights = kernel_matrix(kernels)
    stored = jnp.concatenate([spectra[:, 0, 0], half_spectra[:, 0, 0]], axis=2)
    slabs = []
    for window in range(windows):
        row_owner = owners[window] // width
        held_trial = jnp.where(row_owner[0] == trial_index, 0, 1)
        column = owners[window][held_trial] % width
        arrived = spread(stored[window], TMPL, column)
        crossed = swapped(arrived, "trial", 0)
        kept_slab = jnp.where(held_trial == trial_index, arrived, crossed)
        slabs.append(kept_slab)
    live_mask, source, holder_slot, ranking = read_plan(partners, counts, per_device, width)
    slot_range = jnp.arange(per_device, dtype=jnp.int32)
    cap_range = jnp.arange(capacity, dtype=jnp.int32)
    outgoing = live_mask & (source == device)
    by_rank = outgoing[:, None, :] & (ranking[:, None, :] == cap_range[None, :, None])
    by_slot = holder_slot[:, :, None] == slot_range[None, None, :]
    selector = jnp.einsum("ecs,est->ect", by_rank.astype(jnp.float32), by_slot.astype(jnp.float32))
    selector = selector.reshape(width * capacity, per_device).astype(jnp.bfloat16)
    own_live = live_mask[device]
    incoming = source[device] * capacity + ranking[device]
    receiver = (
        incoming[:, None] == jnp.arange(width * capacity, dtype=jnp.int32)[None, :]
    ) & own_live[:, None]
    receiver = receiver.astype(jnp.bfloat16)
    split_at = bins_whole + tap_count
    flat_kernels = kernels.reshape(per_device, 2 * tap_count)
    outbound = jnp.dot(selector, flat_kernels, preferred_element_type=jnp.float32).astype(
        jnp.bfloat16
    )
    inbound = lax.all_to_all(outbound, TMPL, split_axis=0, concat_axis=0, tiled=True)
    fetched = jnp.dot(receiver, inbound, preferred_element_type=jnp.float32).astype(jnp.bfloat16)
    partner_weights = kernel_matrix(fetched.reshape(per_device, 2, tap_count))
    partner_planes = [
        blocked_powers(partner_weights, slabs[window][:, split_at:], tap_count, bins_half).astype(
            jnp.bfloat16
        )
        for window in range(windows)
    ]
    results = []
    for window in range(windows):
        direct = blocked_powers(weights, slabs[window][:, :split_at], tap_count, bins_whole)
        stretched = jnp.repeat(partner_planes[window], 2, axis=1).astype(jnp.float32)
        summed = jnp.where(own_live[:, None], direct + stretched, jnp.float32(0.0))
        results.append(summed.astype(jnp.bfloat16))
    return jnp.stack(results)[:, None]


def solution(mesh):
    finer = Mesh(
        mesh.devices.reshape(mesh.shape["trial"], 4, 4, 4), ("trial", "tmpl_0", "tmpl_1", "tmpl_2")
    )
    in_specs = (
        P(None, "trial", TMPL, None, None),
        P(None, "trial", TMPL, None, None),
        P(TMPL, None, None),
        P(),
        P(),
        P(),
    )
    out_specs = P(None, "trial", TMPL, None)
    return jax.shard_map(body, mesh=finer, in_specs=in_specs, out_specs=out_specs, check_vma=False)
```

profile of v0, /device:TPU:1, one launch (start us, length us, event | category | flops | bytes accessed | tf_op | source)
XLA Modules:
  0.0 1245.0 jit_solution(4038308129607692235)
XLA Ops:
  12.2 11.9 all-to-all-start
  33.6 39.9 %all-reduce.11.cloned.1.call-done = (bf16[2,25600]{1,0:T(2,128)(2,1)}, bf16[2,25600]{1,0:T(2,128)(2,1)}) async-done(((bf16[2,25600]{1,0:T(2,128)(2,1)}, bf16[2,25600]{1,0:T(2,128)(2,1)}), (bf16[2,25600]{1,0:T(2,128)(2,1)}, bf16[2,25600]{1,0:T(2,128)(2,1)})) %all-reduce.11.cloned.1.call-update) | async-done | bytes 204816 | tf_op jit(solution)/shard_map/psum | solution.py:13
  73.7 43.6 %all-reduce.9.cloned.1.call-done = (bf16[2,25600]{1,0:T(2,128)(2,1)}, bf16[2,25600]{1,0:T(2,128)(2,1)}) async-done(((bf16[2,25600]{1,0:T(2,128)(2,1)}, bf16[2,25600]{1,0:T(2,128)(2,1)}), (bf16[2,25600]{1,0:T(2,128)(2,1)}, bf16[2,25600]{1,0:T(2,128)(2,1)})) %all-reduce.9.cloned.1.call-update) | async-done | bytes 204816 | tf_op jit(solution)/shard_map/psum | solution.py:13
  117.4 44.1 %all-reduce.7.cloned.1.call-done = (bf16[2,25600]{1,0:T(2,128)(2,1)}, bf16[2,25600]{1,0:T(2,128)(2,1)}) async-done(((bf16[2,25600]{1,0:T(2,128)(2,1)}, bf16[2,25600]{1,0:T(2,128)(2,1)}), (bf16[2,25600]{1,0:T(2,128)(2,1)}, bf16[2,25600]{1,0:T(2,128)(2,1)})) %all-reduce.7.cloned.1.call-update) | async-done | bytes 204816 | tf_op jit(solution)/shard_map/psum | solution.py:13
  167.9 163.3 %while.53 = (s32[]{:T(128)}, bf16[16,8192]{1,0:T(8,128)(2,1)S(1)}, bf16[2,8704]{1,0:T(2,128)(2,1)S(1)}, bf16[32,1024]{1,0:T(8,128)(2,1)S(1)}, s32[]{:T(128)}, /*index=5*/s32[]{:T(128)}, s32[]{:T(128)}, s32[]{:T(128)}, s32[]{:T(128)}) while((s32[]{:T(128)}, bf16[16,8192]{1,0:T(8,128)(2,1)S(1)}, bf16[2,8704]{1,0:T(2,128)(2,1)S(1)}, ...), condition=%wide.region_7.8_spmd, body=%wide.region_6.7_spmd.sunk | while | flops 67158024 | bytes 37421308 | solution.py:54
  170.6 4.4 slice.274
  178.8 7.4 reshape.297
  199.3 7.4 reshape.297
  211.4 4.4 slice.274
  219.7 7.4 reshape.297
  240.1 7.4 reshape.297
  260.5 7.4 reshape.297
  272.7 4.4 slice.274
  280.9 7.4 reshape.297
  301.3 7.4 reshape.297
  321.8 7.4 reshape.297
  332.0 173.3 %while.55 = (s32[]{:T(128)}, bf16[16,8192]{1,0:T(8,128)(2,1)}, bf16[2,8704]{1,0:T(2,128)(2,1)}, bf16[32,1024]{1,0:T(8,128)(2,1)S(1)}, s32[]{:T(128)}, /*index=5*/s32[]{:T(128)}, s32[]{:T(128)}, s32[]{:T(128)}, s32[]{:T(128)}) while((s32[]{:T(128)}, bf16[16,8192]{1,0:T(8,128)(2,1)}, bf16[2,8704]{1,0:T(2,128)(2,1)}, ...), condition=%wide.region_14.15_spmd, body=%wide.region_13.14_spmd.sunk | while | flops 67158024 | bytes 37142724 | solution.py:54
  343.8 7.4 reshape.301
  365.5 7.4 reshape.301
  387.1 7.4 reshape.301
  408.7 7.4 reshape.301
  430.4 7.4 reshape.301
  452.0 7.4 reshape.301
  473.7 7.4 reshape.301
  495.3 7.4 reshape.301
  506.4 347.0 %while.52 = (s32[]{:T(128)}, f32[16,16384]{1,0:T(8,128)}, bf16[2,16896]{1,0:T(2,128)(2,1)}, bf16[32,1024]{1,0:T(8,128)(2,1)S(1)}, s32[]{:T(128)}, /*index=5*/s32[]{:T(128)}, s32[]{:T(128)}, s32[]{:T(128)}, s32[]{:T(128)}) while((s32[]{:T(128)}, f32[16,16384]{1,0:T(8,128)}, bf16[2,16896]{1,0:T(2,128)(2,1)}, bf16[32,1024]{1,0:T(8,128)(2,1)S(1)}, ...), condition=%wide.region_4.5_spmd, body=%wide.region_3.4_spmd.sunk | while | flops 67158024 | bytes 37142724 | solution.py:54
  518.4 7.4 reshape.295
  540.0 7.4 reshape.295
  561.7 7.4 reshape.295
  583.4 7.4 reshape.295
  605.0 7.4 reshape.295
  626.7 7.4 reshape.295
  648.3 7.4 reshape.295
  670.0 7.4 reshape.295
  691.7 7.4 reshape.295
  713.3 7.4 reshape.295
  735.0 7.4 reshape.295
  756.6 7.4 reshape.295
  778.3 7.4 reshape.295
  800.0 7.4 reshape.295
  821.6 7.4 reshape.295
  843.3 7.4 reshape.295
  854.4 335.7 %while.54 = (s32[]{:T(128)}, f32[16,16384]{1,0:T(8,128)}, bf16[2,16896]{1,0:T(2,128)(2,1)S(1)}, bf16[32,1024]{1,0:T(8,128)(2,1)S(1)}, s32[]{:T(128)}, /*index=5*/s32[]{:T(128)}, s32[]{:T(128)}, s32[]{:T(128)}, s32[]{:T(128)}) while((s32[]{:T(128)}, f32[16,16384]{1,0:T(8,128)}, bf16[2,16896]{1,0:T(2,128)(2,1)S(1)}, ...), condition=%wide.region_12.13_spmd, body=%wide.region_11.12_spmd.sunk | while | flops 67158024 | bytes 37142724 | solution.py:54
  865.5 7.4 reshape.299
  886.5 7.4 reshape.299
  907.4 7.4 reshape.299
  928.4 7.4 reshape.299
  949.4 7.4 reshape.299
  970.4 7.4 reshape.299
  991.3 7.4 reshape.299
  1012.3 7.4 reshape.299
  1033.3 7.4 reshape.299
  1054.2 7.4 reshape.299
  1075.2 7.4 reshape.299
  1096.2 7.4 reshape.299
  1117.2 7.4 reshape.299
  1138.1 7.4 reshape.299
  1159.1 7.4 reshape.299
  1180.0 7.4 reshape.299
  1194.9 4.6 copy.84
  1199.5 4.9 copy.81
  1204.4 8.5 broadcast_in_dim.106
  1212.9 4.6 broadcast_in_dim.107
  1217.5 12.7 %fusion.8 = (bf16[1,16,16384]{1,2,0:T(8,128)(2,1)}, bf16[1,16,16384]{1,2,0:T(8,128)(2,1)}) fusion(f32[16,16384]{0,1:T(8,128)} %copy.81, f32[16,16384]{0,1:T(8,128)} %bitcast.153, pred[16]{0:T(512)(128)(4,1)S(1)} %copy-done.10, f32[16,16384]{0,1:T(8,128)S(1)} %bitcast.152, f32[16,16384]{0,1:T(8,128)} %bitcast.154), kind=kLoop, calls=%fused_computation.30 | loop fusion | flops 1572864 | bytes 5242896 | tf_op jit(solution)/shard_map/stack | solution.py:124
  (542 shorter events, 684.3 us)
Async XLA Ops:
  12.2 21.1 %all-to-all-start = ((bf16[64,2,512]{2,1,0:T(2,128)(2,1)}), bf16[64,2,512]{2,1,0:T(2,128)(2,1)S(1)}, u32[]{:S(2)}, u32[]{:S(2)}) async-start(bf16[64,2,512]{2,1,0:T(2,128)(2,1)} %reshape.284), calls=%async_computation | async-start | bytes 262144 | tf_op jit(solution)/shard_map/all_to_all | solution.py:109
  24.2 49.4 %all-reduce.11.cloned.1.call-start = ((), (), s32[]{:S(2)}) async-start(), calls=%async_computation.3 | async-start | bytes 409600 | tf_op jit(solution)/shard_map/psum | solution.py:13
  31.9 85.4 %all-reduce.9.cloned.1.call-start = ((), (), s32[]{:S(2)}) async-start(), calls=%async_computation.2 | async-start | bytes 409600 | tf_op jit(solution)/shard_map/psum | solution.py:13
  33.1 134.8 %copy-start.9 = (pred[16]{0:T(512)(128)(4,1)}, pred[16]{0:T(512)(128)(4,1)S(1)}, u32[]{:S(2)}) copy-start(pred[16]{0:T(512)(128)(4,1)S(1)} %dynamic-slice_reduce_fusion) | copy-start | bytes 52
  73.6 87.9 %all-reduce.7.cloned.1.call-start = ((), (), s32[]{:S(2)}) async-start(), calls=%async_computation.1 | async-start | bytes 409600 | tf_op jit(solution)/shard_map/psum | solution.py:13
  161.5 3.9 collective-permute-start.1
  164.2 2.8 collective-permute-start
  167.9 2.7 copy-start.7
  186.2 2.1 copy-start.8
  188.3 2.7 copy-start.7
  206.6 1.6 slice-start
  206.6 2.1 copy-start.8
  208.7 2.7 copy-start.7
  227.0 2.1 copy-start.8
  229.1 2.7 copy-start.7
  247.5 1.6 slice-start
  247.5 2.1 copy-start.8
  249.6 2.7 copy-start.7
  267.9 1.6 slice-start
  267.9 2.1 copy-start.8
  270.0 2.7 copy-start.7
  288.3 2.1 copy-start.8
  290.4 2.7 copy-start.7
  308.7 2.1 copy-start.8
  310.8 2.7 copy-start.7
  329.1 1.6 slice-start
  329.1 2.1 copy-start.8
  372.8 1.6 slice-start.1
  394.5 1.6 slice-start.1
  459.4 1.6 slice-start.1
  481.0 1.6 slice-start.1
  502.7 1.6 slice-start.1
  506.4 348.0 %slice-start.6 = ((bf16[2,25600]{1,0:T(2,128)(2,1)}), bf16[2,16896]{1,0:T(2,128)(2,1)S(1)}, s32[]{:S(2)}) async-start(bf16[2,25600]{1,0:T(2,128)(2,1)} %copy-done.6), calls=%async_computation.10 | async-start | bytes 135168 | tf_op jit(solution)/shard_map/slice | solution.py:120
  525.7 1.6 slice-start.2
  547.4 1.6 slice-start.2
  569.1 1.6 slice-start.2
  590.7 1.6 slice-start.2
  612.4 1.6 slice-start.2
  634.0 1.6 slice-start.2
  720.7 1.6 slice-start.2
  785.7 1.6 slice-start.2
  807.3 1.6 slice-start.2
  829.0 1.6 slice-start.2
  850.6 1.6 slice-start.2
  854.4 335.7 %copy-start.5 = (bf16[16,8192]{1,0:T(8,128)(2,1)S(1)}, bf16[16,8192]{1,0:T(8,128)(2,1)}, u32[]{:S(2)}) copy-start(bf16[16,8192]{1,0:T(8,128)(2,1)} %get-tuple-element.324) | copy-start | bytes 786436
  872.8 1.6 slice-start.3
  893.8 1.6 slice-start.3
  914.8 1.6 slice-start.3
  935.8 1.6 slice-start.3
  977.7 1.6 slice-start.3
  998.7 1.6 slice-start.3
  1019.7 1.6 slice-start.3
  1040.6 1.6 slice-start.3
  1061.6 1.6 slice-start.3
  1082.6 1.6 slice-start.3
  1103.5 1.6 slice-start.3
  1145.5 1.6 slice-start.3
  1190.1 2.4 copy-start.4
  1192.5 2.4 copy-start.1
  1194.9 4.6 copy-start.2
  1204.4 8.5 copy-start
  1204.4 13.1 %slice-start.4 = ((s8[8388608]{0:T(1024)(128)(4,1)}), s8[4194304]{0:T(1024)(128)(4,1)S(1)}, s32[]{:S(2)}) async-start(s8[8388608]{0:T(1024)(128)(4,1)} %bitcast.151), calls=%async_computation.8 | async-start | bytes 8388608
  1212.9 4.6 slice-start.5
  1212.9 4.6 copy-start.10
  (18 other events, 27.1 us)
Sparse Core Ops, SparseCore 0:
  32.0 41.4 all-reduce.10
  76.0 41.3 all-reduce.8
  119.8 41.6 all-reduce.6
where the time goes:
time: 1250 us; the launch traced here: 1240 us
  local copies, waits for them, and re-layouts  1010 us (81%)
  waiting for transfers between devices  129 us (10%)
  other arithmetic  45.8 us (4%)
  matrix products  23 us (2%)
  between operations  17.3 us (1%)
  starting transfers between devices  15 us (1%)
    reshape x48, local copies, waits for them, and re-layouts, hankel_rows(): repeated[:, :tap_count * (length + 1)].reshape(2, tap_count, length + 1)  353 us
    while x176, local copies, waits for them, and re-layouts  313 us
    slice x48, local copies, waits for them, and re-layouts, hankel_rows(): repeated[:, :tap_count * (length + 1)].reshape(2, tap_count, length + 1)  209 us
    psum x3, waiting for transfers between devices, spread(): x = lax.psum(x, axis)  128 us
    slice x96, local copies, waits for them, and re-layouts, hankel_rows(): return skewed[:, :, :columns].reshape(2 * tap_count, columns)  76.3 us
    dynamic_update_slice x48, other arithmetic, add_block(): return lax.dynamic_update_slice_in_dim(result, values, first_bin, 1)  25.9 us
  transfers between devices with their start and end apart: 6, of which 4 were waited for; matrix products, arithmetic and copies ran while one was open for 1% of the time, Pallas kernels for 0%

commit v1 on v0

v1 whole, which is shorter than its diff:
```python
import jax
import jax.numpy as jnp
from jax import lax
from jax.experimental import pallas as pl
from jax.experimental.pallas import tpu as pltpu
from jax.sharding import Mesh
from jax.sharding import PartitionSpec as P

TMPL = ("tmpl_0", "tmpl_1", "tmpl_2")
F32 = jnp.float32
BF = jnp.bfloat16
VMEM = pl.BlockSpec(memory_space=pltpu.VMEM)
SMEM = pl.BlockSpec(memory_space=pltpu.SMEM)


def swapped(x):
    return lax.ppermute(x, "trial", [(0, 1), (1, 0)])


def pack_kernel(owners_ref, part_ref, k_ref, x_ref, y_ref, xc_ref, yc_ref, op_ref, rev_ref):
    me = lax.axis_index(TMPL)
    r0 = lax.broadcasted_iota(jnp.int32, (128, 128), 0)
    c0 = lax.broadcasted_iota(jnp.int32, (128, 128), 1)
    flip = (r0 == (128 - c0) % 128).astype(BF)
    rev = jnp.dot(k_ref[...], flip, preferred_element_type=F32).astype(BF)
    rev_ref[...] = rev
    wanted = jnp.concatenate(
        [
            (jnp.broadcast_to(part_ref[r : r + 1, :], (128, 128)) == me * 16 + r0 // 8).astype(BF)
            for r in range(8)
        ],
        axis=0,
    )
    group = (
        lax.broadcasted_iota(jnp.int32, (64, 128), 0) // 8
        == lax.broadcasted_iota(jnp.int32, (64, 128), 1) // 16
    ).astype(BF)
    hit = lax.dot_general(group, wanted, (((1,), (1,)), ((), ())), preferred_element_type=F32)
    same = (
        lax.broadcasted_iota(jnp.int32, (64, 128), 0) % 8
        == lax.broadcasted_iota(jnp.int32, (64, 128), 1) % 8
    )
    for r in range(8):
        pick = jnp.where(same, hit[:, r * 128 : (r + 1) * 128], 0.0).astype(BF)
        sent = jnp.dot(pick, rev, preferred_element_type=F32)
        op_ref[8 * r : 8 * r + 8, 0:8, :] = sent.reshape(8, 8, 128).astype(BF)
    op_ref[50:64, 8:24, :] = jnp.zeros((14, 16, 128), BF)
    for w in range(2):
        rows = slice(8 + 8 * w, 16 + 8 * w)
        crossed = owners_ref[w, 0] >= 64

        @pl.when(crossed)
        def _():
            op_ref[0:33, rows, :] = xc_ref[w]
            op_ref[33:50, rows, :] = yc_ref[w]

        @pl.when(jnp.logical_not(crossed))
        def _():
            op_ref[0:33, rows, :] = x_ref[w]
            op_ref[33:50, rows, :] = y_ref[w]


def relay_kernel(owners_ref, part_ref, got_ref, out_ref, h_ref):
    me = lax.axis_index(TMPL)
    row = lax.axis_index("trial")
    for w in range(2):
        block = got_ref[owners_ref[w, row] % 64, 8 + 8 * w : 16 + 8 * w, :]
        out_ref[:, 8 * w : 8 * w + 8, :] = jnp.broadcast_to(block[None], (64, 8, 128))
    for s in range(16):
        source = jnp.maximum(part_ref[me * 16 + s], 0) // 16
        h_ref[s] = got_ref[source, 0:8, :]


def correlate_kernel(counts_ref, g_ref, rev_ref, hrev_ref, out_ref, flat, y64, lx, ly, revf, hrevf, ra, rb, pa, pb, scr):
    me = lax.axis_index(TMPL)
    L=128
    for w in range(2):
        flat[w] = g_ref[:, 8*w:8*w+8, :].astype(F32).reshape(512, L)
    revf[...] = rev_ref[...].astype(F32)
    hrevf[...] = hrev_ref[...].astype(F32)
    lane=lax.broadcasted_iota(jnp.int32,(68,L),1)
    for w in range(2):
        for c in range(2):
            for q in range(5):
                lx[w*128:(w+1)*128, (c*5+q)*L:(c*5+q+1)*L] = flat[w, pl.ds(2*q+c,128,stride=2), :].astype(BF)
            even = flat[w, pl.ds(264+c,68,stride=2), :]
            nxt = flat[w, pl.ds(266+c,68,stride=2), :]
            odd = jnp.where(lane<64, pltpu.roll(even,64,1), pltpu.roll(nxt,64,1))
            y64[pl.ds(0,68,stride=2), :] = even
            y64[pl.ds(1,68,stride=2), :] = odd
            for q in range(5):
                ly[w*128:(w+1)*128, (c*5+q)*L:(c*5+q+1)*L] = y64[2*q:2*q+128, :].astype(BF)
    tri = lax.broadcasted_iota(jnp.int32,(L,L),0) >= lax.broadcasted_iota(jnp.int32,(L,L),1)
    left = lax.broadcasted_iota(jnp.int32,(L,L),1) < 64
    zero = jnp.zeros((L,L),F32)
    live_n = counts_ref[me]
    def circ(ref, row):
        v = jnp.broadcast_to(ref[pl.ds(row,1), :], (L,L))
        return pltpu.roll(v, 0, 1, stride=1, stride_axis=0)
    def tiles(cs):
        return [jnp.where(tri,cs[0],zero)]+[jnp.where(tri,cs[q],cs[q-1]) for q in (1,2,3)]+[jnp.where(tri,zero,cs[3])]
    def put(dst, re, im):
        for q in range(5):
            r = re[q].astype(BF); i = im[q].astype(BF)
            dst[q*L:(q+1)*L, 0:L] = r
            dst[q*L:(q+1)*L, L:2*L] = i
            dst[(5+q)*L:(6+q)*L, 0:L] = -i
            dst[(5+q)*L:(6+q)*L, L:2*L] = r
    def build(pair, r_refs, p_ref):
        for k in range(2):
            t = 2*pair+k
            put(r_refs[k], *[tiles([circ(revf, t*8+2*q+c) for q in range(4)]) for c in range(2)])
        h=[]
        for c in range(2):
            a = [circ(hrevf, (2*pair)*8+2*q+c) for q in range(4)]
            bb = [pltpu.roll(jnp.broadcast_to(hrevf[pl.ds((2*pair+1)*8+2*q+c,1), :],(L,L)),64,1,stride=1,stride_axis=0) for q in range(4)]
            m = [jnp.where(left, a[q], bb[q]) for q in range(4)]
            trc = lax.broadcasted_iota(jnp.int32,(L,L),0) >= lax.broadcasted_iota(jnp.int32,(L,L),1) % 64
            h.append([jnp.where(trc,m[0],zero)]+[jnp.where(trc,m[q],m[q-1]) for q in (1,2,3)]+[jnp.where(trc,zero,m[3])])
        put(p_ref, *h)
    er = lax.broadcasted_iota(jnp.int32,(L,2*L),0); ec = lax.broadcasted_iota(jnp.int32,(L,2*L),1)
    dup = (er == (ec//128)*64 + (ec%128)//2).astype(BF)
    def work(pair, r_refs, p_ref):
        z = jnp.dot(ly[...], p_ref[...], preferred_element_type=F32)
        plane = (z[:, :L]*z[:, :L] + z[:, L:]*z[:, L:]).astype(BF)
        wide = jnp.dot(plane, dup, preferred_element_type=F32)
        for k in range(2):
            t = 2*pair+k
            d = jnp.dot(lx[...], r_refs[k][...], preferred_element_type=F32)
            tot = d[:, :L]*d[:, :L] + d[:, L:]*d[:, L:] + wide[:, k*L:(k+1)*L]
            tot = jnp.where(t < live_n, tot, 0.0)
            scr[:, pl.ds(t,1), :] = tot.reshape(256,1,L)
    A=((ra.at[0],ra.at[1]),pa); B=((rb.at[0],rb.at[1]),pb)
    build(0,*A)
    def step(i,_):
        work(2*i,*A); build(2*i+1,*B)
        work(2*i+1,*B); build(jnp.minimum(2*i+2,7),*A)
        return 0
    lax.fori_loop(0,4,step,0)
    for w in range(2):
        def pk(a,_):
            out_ref[w, :, pl.ds(pl.multiple_of(a*L,L),L)] = scr[w*128+a].astype(BF)
            return 0
        lax.fori_loop(0,128,pk,0,unroll=8)


def body(spectra, half_spectra, kernels, owners, counts, partners):
    x = spectra.reshape(2, 2, 132, 128).transpose(0, 2, 1, 3).reshape(2, 33, 8, 128)
    y = half_spectra.reshape(2, 2, 68, 128).transpose(0, 2, 1, 3).reshape(2, 17, 8, 128)
    k = kernels.reshape(16, 2, 4, 128).transpose(0, 2, 1, 3).reshape(128, 128)
    xc, yc = swapped(x), swapped(y)
    sent, rev = pl.pallas_call(
        pack_kernel,
        out_shape=(
            jax.ShapeDtypeStruct((64, 24, 128), BF),
            jax.ShapeDtypeStruct((128, 128), BF),
        ),
        in_specs=[SMEM] + [VMEM] * 6,
        out_specs=(VMEM, VMEM),
        name="pack",
    )(owners, partners.reshape(8, 128), k, x, y, xc, yc)
    got = lax.all_to_all(sent, TMPL, 0, 0, tiled=True)
    repeated, h = pl.pallas_call(
        relay_kernel,
        out_shape=(
            jax.ShapeDtypeStruct((64, 16, 128), BF),
            jax.ShapeDtypeStruct((16, 8, 128), BF),
        ),
        in_specs=[SMEM, SMEM, VMEM],
        out_specs=(VMEM, VMEM),
        name="relay",
    )(owners, partners, got)
    whole = lax.all_to_all(repeated, TMPL, 0, 0, tiled=True)
    out = pl.pallas_call(
        correlate_kernel,
        out_shape=jax.ShapeDtypeStruct((2, 16, 16384), BF),
        in_specs=[SMEM] + [VMEM] * 3,
        out_specs=VMEM,
        scratch_shapes=[
            pltpu.VMEM((2, 512, 128), F32),
            pltpu.VMEM((136, 128), F32),
            pltpu.VMEM((256, 1280), BF),
            pltpu.VMEM((256, 1280), BF),
            pltpu.VMEM((128, 128), F32),
            pltpu.VMEM((128, 128), F32),
            pltpu.VMEM((2, 1280, 256), BF),
            pltpu.VMEM((2, 1280, 256), BF),
            pltpu.VMEM((1280, 256), BF),
            pltpu.VMEM((1280, 256), BF),
            pltpu.VMEM((256, 16, 128), F32),
        ],
        name="correlate",
    )(counts, whole, rev, h.reshape(128, 128))
    return out[:, None]


def solution(mesh):
    finer = Mesh(
        mesh.devices.reshape(mesh.shape["trial"], 4, 4, 4), ("trial", "tmpl_0", "tmpl_1", "tmpl_2")
    )
    in_specs = (
        P(None, "trial", TMPL, None, None),
        P(None, "trial", TMPL, None, None),
        P(TMPL, None, None),
        P(),
        P(),
        P(),
    )
    out_specs = P(None, "trial", TMPL, None)
    return jax.shard_map(body, mesh=finer, in_specs=in_specs, out_specs=out_specs, check_vma=False)
```

time: 1250 us -> 59.1 us (0.05)
  the two profiles are of different devices: /device:TPU:1 before, /device:TPU:0 now
where the time goes in v1:
time: 59.1 us; the launch traced here: 58.7 us
  blocking collectives  39.8 us (67%)
  Pallas kernels  14.9 us (25%)
  local copies, waits for them, and re-layouts  2.54 us (4%)
  waiting for transfers between devices  1.25 us (2%)
    all_to_all x1, blocking collectives, body(): got = lax.all_to_all(sent, TMPL, 0, 0, tiled=True)  23.9 us
    all_to_all x1, blocking collectives, body(): whole = lax.all_to_all(repeated, TMPL, 0, 0, tiled=True)  15.9 us
    pallas_call x1, Pallas kernels, body(): pl.pallas_call(correlate_kernel, out_shape=jax.ShapeDtypeStruct((2, 16, 1...  10.9 us
    pallas_call x1, Pallas kernels, body(): pl.pallas_call(pack_kernel, out_shape=(jax.ShapeDtypeStruct((64, 24, 128)...  2.26 us
    pallas_call x1, Pallas kernels, body(): pl.pallas_call(relay_kernel, out_shape=(jax.ShapeDtypeStruct((64, 16, 128...  1.79 us
    unnamed x10, local copies, waits for them, and re-layouts  1.34 us
    ppermute x2, waiting for transfers between devices, swapped(): return lax.ppermute(x, 'trial', [(0, 1), (1, 0)])  1.25 us
  transfers between devices with their start and end apart: 2, of which 1 were waited for; matrix products, arithmetic and copies ran while one was open for 0% of the time, Pallas kernels for 0%

profile of v1, /device:TPU:0, one launch (start us, length us, event | category | flops | bytes accessed | tf_op | source)
XLA Modules:
  0.0 58.7 jit_solution(7981004743817558757)
XLA Ops:
  0.0 1.0 %reshape.27 = bf16[2,2,132,128]{3,2,1,0:T(8,128)(2,1)S(1)} reshape(bf16[2,1,1,2,16896]{4,3,2,1,0:T(2,128)(2,1)} %param.6) | data formatting | bytes 270336 | tf_op jit(solution)/shard_map/reshape | solution.py:148
  1.0 0.0 copy-start.4
  1.0 0.1 copy.12
  1.1 0.0 copy-start
  1.1 0.1 collective-permute-start
  1.2 0.7 %copy-done.4 = bf16[2,1,1,2,8704]{4,3,2,1,0:T(2,128)(2,1)S(1)} copy-done((bf16[2,1,1,2,8704]{4,3,2,1,0:T(2,128)(2,1)S(1)}, bf16[2,1,1,2,8704]{4,3,2,1,0:T(2,128)(2,1)}, u32[]{:S(2)}) %copy-start.4) | copy-done | bytes 69656
  1.9 0.1 copy.13
  2.0 0.0 copy-done
  2.0 0.0 copy-start.1
  2.0 0.1 collective-permute-start.1
  2.1 1.2 %collective-permute-done.1.yc_ref = bf16[2,17,8,128]{3,2,1,0:T(8,128)(2,1)S(1)} collective-permute-done((bf16[2,17,8,128]{3,2,1,0:T(8,128)(2,1)S(1)}, bf16[2,17,8,128]{3,2,1,0:T(8,128)(2,1)S(1)}, u32[]{:S(2)}, u32[]{:S(2)}) %collective-permute-start.1) | collective-permute-done | bytes 69664 | tf_op jit(solution)/shard_map/ppermute | solution.py:17
  3.4 0.0 copy-start.3
  3.4 0.0 collective-permute-done.xc_ref
  3.4 0.0 copy-start.2
  3.4 0.0 copy-done.1
  3.4 0.6 %copy-done.3 = bf16[2,17,8,128]{3,2,1,0:T(8,128)(2,1)} copy-done((bf16[2,17,8,128]{3,2,1,0:T(8,128)(2,1)}, bf16[2,17,8,128]{3,2,1,0:T(8,128)(2,1)S(1)}, u32[]{:S(2)}) %copy-start.3) | copy-done | bytes 69656
  4.0 0.1 copy-done.2
  4.0 2.3 %pack.1 = (bf16[64,24,128]{2,1,0:T(8,128)(2,1)}, bf16[128,128]{1,0:T(8,128)(2,1)}) custom-call(s32[2,2]{1,0:T(2,128)} %owners_ref.3, s32[8,128]{1,0:T(8,128)} %bitcast.22, bf16[128,128]{1,0:T(8,128)(2,1)} %bitcast.20, bf16[2,33,8,128]{3,2,1,0:T(8,128)(2,1)} %bitcast.16, bf16[2,17,8,128]{3,2,1,0:T(8,128)(2,1)} %bitcast.19, bf16[2,33,8,128]{3,2,1,0:T(8,128)(2,1)} %copy-done.2, ...), custom_call_target="tpu_custom_call" | custom-call | tf_op jit(solution)/shard_map/pack/pallas_call | solution.py:152
  6.3 23.9 %all_to_all.10.got_ref = bf16[64,24,128]{2,1,0:T(8,128)(2,1)} all-to-all(bf16[64,24,128]{2,1,0:T(8,128)(2,1)} %get-tuple-element.9), channel_id=1, replica_groups=mesh['trial'=2,'tmpl_0'=4,'tmpl_1'=4,'tmpl_2'=4] {'tmpl_0','tmpl_1','tmp..., dimensions={0} | all-to-all | bytes 786432 | tf_op jit(solution)/shard_map/all_to_all | solution.py:162
  30.2 1.8 %relay.1 = (bf16[64,16,128]{2,1,0:T(8,128)(2,1)}, bf16[16,8,128]{2,1,0:T(8,128)(2,1)}) custom-call(s32[2,2]{1,0:T(2,128)} %owners_ref.3, s32[1024]{0:T(1024)} %part_ref.1, bf16[64,24,128]{2,1,0:T(8,128)(2,1)} %all_to_all.10.got_ref), custom_call_target="tpu_custom_call" | custom-call | tf_op jit(solution)/shard_map/relay/pallas_call | solution.py:163
  31.9 15.9 %all_to_all.11.g_ref = bf16[64,16,128]{2,1,0:T(8,128)(2,1)} all-to-all(bf16[64,16,128]{2,1,0:T(8,128)(2,1)} %get-tuple-element.10), channel_id=1, replica_groups=mesh['trial'=2,'tmpl_0'=4,'tmpl_1'=4,'tmpl_2'=4] {'tmpl_0','tmpl_1','tmp..., dimensions={0} | all-to-all | bytes 524288 | tf_op jit(solution)/shard_map/all_to_all | solution.py:173
  47.9 10.9 %correlate.1 = bf16[2,16,16384]{2,1,0:T(8,128)(2,1)} custom-call(s32[64]{0:T(128)} %counts_ref.1, bf16[64,16,128]{2,1,0:T(8,128)(2,1)} %all_to_all.11.g_ref, bf16[128,128]{1,0:T(8,128)(2,1)} %get-tuple-element.11.rev_ref, bf16[128,128]{1,0:T(8,128)(2,1)} %bitcast.21), custom_call_target="tpu_custom_call" | custom-call | tf_op jit(solution)/shard_map/correlate/pallas_call | solution.py:174
  (1 shorter events, 0.0 us)
Async XLA Ops:
  1.0 0.9 %copy-start.4 = (bf16[2,1,1,2,8704]{4,3,2,1,0:T(2,128)(2,1)S(1)}, bf16[2,1,1,2,8704]{4,3,2,1,0:T(2,128)(2,1)}, u32[]{:S(2)}) copy-start(bf16[2,1,1,2,8704]{4,3,2,1,0:T(2,128)(2,1)} %param.7) | copy-start | bytes 208900
  1.1 0.9 %copy-start = (bf16[2,132,2,128]{3,2,1,0:T(2,128)(2,1)}, bf16[2,132,2,128]{3,2,1,0:T(2,128)(2,1)S(1)}, u32[]{:S(2)}) copy-start(bf16[2,132,2,128]{3,2,1,0:T(2,128)(2,1)S(1)} %copy.12) | copy-start | bytes 405508
  1.1 2.2 %collective-permute-start = (bf16[2,33,8,128]{3,2,1,0:T(8,128)(2,1)S(1)}, bf16[2,33,8,128]{3,2,1,0:T(8,128)(2,1)S(1)}, u32[]{:S(2)}, u32[]{:S(2)}) collective-permute-start(bf16[2,33,8,128]{3,2,1,0:T(8,128)(2,1)S(1)} %bitcast.15), channel_id=1, source_target_pairs={{0,64},{64,0},{1,65},{65,1},{2,66},{66,2},{3,67},{67,3},{4,68},{68... | collective-permute-start | bytes 405512 | tf_op jit(solution)/shard_map/ppermute | solution.py:17
  2.0 1.4 %copy-start.1 = (bf16[2,68,2,128]{3,2,1,0:T(2,128)(2,1)}, bf16[2,68,2,128]{3,2,1,0:T(2,128)(2,1)S(1)}, u32[]{:S(2)}) copy-start(bf16[2,68,2,128]{3,2,1,0:T(2,128)(2,1)S(1)} %copy.13) | copy-start | bytes 208900
  2.0 1.3 %collective-permute-start.1 = (bf16[2,17,8,128]{3,2,1,0:T(8,128)(2,1)S(1)}, bf16[2,17,8,128]{3,2,1,0:T(8,128)(2,1)S(1)}, u32[]{:S(2)}, u32[]{:S(2)}) collective-permute-start(bf16[2,17,8,128]{3,2,1,0:T(8,128)(2,1)S(1)} %bitcast.18), channel_id=1, source_target_pairs={{0,64},{64,0},{1,65},{65,1},{2,66},{66,2},{3,67},{67,3},{4,68},{68... | collective-permute-start | bytes 208904 | tf_op jit(solution)/shard_map/ppermute | solution.py:17
  3.4 0.6 %copy-start.3 = (bf16[2,17,8,128]{3,2,1,0:T(8,128)(2,1)}, bf16[2,17,8,128]{3,2,1,0:T(8,128)(2,1)S(1)}, u32[]{:S(2)}) copy-start(bf16[2,17,8,128]{3,2,1,0:T(8,128)(2,1)S(1)} %collective-permute-done.1.yc_ref) | copy-start | bytes 208900
  3.4 0.7 %copy-start.2 = (bf16[2,33,8,128]{3,2,1,0:T(8,128)(2,1)}, bf16[2,33,8,128]{3,2,1,0:T(8,128)(2,1)S(1)}, u32[]{:S(2)}) copy-start(bf16[2,33,8,128]{3,2,1,0:T(8,128)(2,1)S(1)} %collective-permute-done.xc_ref) | copy-start | bytes 405508

commit v2 on v1

--- a/solution.py
+++ b/solution.py
@@ -145,8 +145,8 @@
 
 
 def body(spectra, half_spectra, kernels, owners, counts, partners):
-    x = spectra.reshape(2, 2, 132, 128).transpose(0, 2, 1, 3).reshape(2, 33, 8, 128)
-    y = half_spectra.reshape(2, 2, 68, 128).transpose(0, 2, 1, 3).reshape(2, 17, 8, 128)
+    x = spectra.reshape(2, 2, 33, 4, 128).transpose(0, 2, 3, 1, 4).reshape(2, 33, 8, 128)
+    y = half_spectra.reshape(2, 2, 17, 4, 128).transpose(0, 2, 3, 1, 4).reshape(2, 17, 8, 128)
     k = kernels.reshape(16, 2, 4, 128).transpose(0, 2, 1, 3).reshape(128, 128)
     xc, yc = swapped(x), swapped(y)
     sent, rev = pl.pallas_call(

time: 59.1 us -> 57.5 us (0.973)
  local copies, waits for them, and re-layouts: 2.54 us -> 0.67 us
    reshape x2 -> x0, local copies, waits for them, and re-layouts: 1.04 us -> none  [the longest x1 0.99 us: body(): spectra.reshape(2, 2, 132, 128).transpose(0, 2, 1, 3).reshape(2, 33, 8, 128)]
    unnamed x10 -> x4, local copies, waits for them, and re-layouts: 1.34 us -> 0.67 us
where the time goes in v2:
time: 57.5 us; the launch traced here: 57.2 us
  blocking collectives  40 us (70%)
  Pallas kernels  14.9 us (26%)
  waiting for transfers between devices  1.16 us (2%)
  local copies, waits for them, and re-layouts  0.67 us (1%)
    all_to_all x1, blocking collectives, body(): got = lax.all_to_all(sent, TMPL, 0, 0, tiled=True)  24 us
    all_to_all x1, blocking collectives, body(): whole = lax.all_to_all(repeated, TMPL, 0, 0, tiled=True)  15.9 us
    pallas_call x1, Pallas kernels, body(): pl.pallas_call(correlate_kernel, out_shape=jax.ShapeDtypeStruct((2, 16, 1...  10.9 us
    pallas_call x1, Pallas kernels, body(): pl.pallas_call(pack_kernel, out_shape=(jax.ShapeDtypeStruct((64, 24, 128)...  2.26 us
    pallas_call x1, Pallas kernels, body(): pl.pallas_call(relay_kernel, out_shape=(jax.ShapeDtypeStruct((64, 16, 128...  1.79 us
    ppermute x2, waiting for transfers between devices, swapped(): return lax.ppermute(x, 'trial', [(0, 1), (1, 0)])  1.16 us
  transfers between devices with their start and end apart: 2, of which 1 were waited for; matrix products, arithmetic and copies ran while one was open for 0% of the time, Pallas kernels for 0%

profile of v2, /device:TPU:0, one launch (start us, length us, event | category | flops | bytes accessed | tf_op | source)
XLA Modules:
  0.0 57.2 jit_solution(7776488159226931971)
XLA Ops:
  0.0 0.0 collective-permute-start
  0.0 0.5 collective-permute-start.1
  0.5 1.2 %collective-permute-done.1.yc_ref = bf16[2,17,8,128]{3,2,1,0:T(8,128)(2,1)S(1)} collective-permute-done((bf16[2,17,8,128]{3,2,1,0:T(8,128)(2,1)}, bf16[2,17,8,128]{3,2,1,0:T(8,128)(2,1)S(1)}, u32[]{:S(2)}, u32[]{:S(2)}) %collective-permute-start.1) | collective-permute-done | bytes 69664 | tf_op jit(solution)/shard_map/ppermute | solution.py:17
  1.7 0.0 copy-start.1
  1.7 0.0 collective-permute-done.xc_ref
  1.7 0.0 copy-start
  1.7 0.6 %copy-done.1 = bf16[2,17,8,128]{3,2,1,0:T(8,128)(2,1)} copy-done((bf16[2,17,8,128]{3,2,1,0:T(8,128)(2,1)}, bf16[2,17,8,128]{3,2,1,0:T(8,128)(2,1)S(1)}, u32[]{:S(2)}) %copy-start.1) | copy-done | bytes 69656
  2.3 0.1 copy-done
  2.3 2.3 %pack.1 = (bf16[64,24,128]{2,1,0:T(8,128)(2,1)}, bf16[128,128]{1,0:T(8,128)(2,1)}) custom-call(s32[2,2]{1,0:T(2,128)} %owners_ref.3, s32[8,128]{1,0:T(8,128)} %bitcast.26, bf16[128,128]{1,0:T(8,128)(2,1)} %bitcast.24, bf16[2,33,8,128]{3,2,1,0:T(8,128)(2,1)} %bitcast.21, bf16[2,17,8,128]{3,2,1,0:T(8,128)(2,1)} %bitcast.23, bf16[2,33,8,128]{3,2,1,0:T(8,128)(2,1)} %copy-done, ...), custom_call_target="tpu_custom_call" | custom-call | tf_op jit(solution)/shard_map/pack/pallas_call | solution.py:152
  4.6 24.0 %all_to_all.10.got_ref = bf16[64,24,128]{2,1,0:T(8,128)(2,1)} all-to-all(bf16[64,24,128]{2,1,0:T(8,128)(2,1)} %get-tuple-element.9), channel_id=1, replica_groups=mesh['trial'=2,'tmpl_0'=4,'tmpl_1'=4,'tmpl_2'=4] {'tmpl_0','tmpl_1','tmp..., dimensions={0} | all-to-all | bytes 786432 | tf_op jit(solution)/shard_map/all_to_all | solution.py:162
  28.6 1.8 %relay.1 = (bf16[64,16,128]{2,1,0:T(8,128)(2,1)}, bf16[16,8,128]{2,1,0:T(8,128)(2,1)}) custom-call(s32[2,2]{1,0:T(2,128)} %owners_ref.3, s32[1024]{0:T(1024)} %part_ref.1, bf16[64,24,128]{2,1,0:T(8,128)(2,1)} %all_to_all.10.got_ref), custom_call_target="tpu_custom_call" | custom-call | tf_op jit(solution)/shard_map/relay/pallas_call | solution.py:163
  30.4 15.9 %all_to_all.11.g_ref = bf16[64,16,128]{2,1,0:T(8,128)(2,1)} all-to-all(bf16[64,16,128]{2,1,0:T(8,128)(2,1)} %get-tuple-element.10), channel_id=1, replica_groups=mesh['trial'=2,'tmpl_0'=4,'tmpl_1'=4,'tmpl_2'=4] {'tmpl_0','tmpl_1','tmp..., dimensions={0} | all-to-all | bytes 524288 | tf_op jit(solution)/shard_map/all_to_all | solution.py:173
  46.4 10.9 %correlate.1 = bf16[2,16,16384]{2,1,0:T(8,128)(2,1)} custom-call(s32[64]{0:T(128)} %counts_ref.1, bf16[64,16,128]{2,1,0:T(8,128)(2,1)} %all_to_all.11.g_ref, bf16[128,128]{1,0:T(8,128)(2,1)} %get-tuple-element.11.rev_ref, bf16[128,128]{1,0:T(8,128)(2,1)} %bitcast.25), custom_call_target="tpu_custom_call" | custom-call | tf_op jit(solution)/shard_map/correlate/pallas_call | solution.py:174
Async XLA Ops:
  0.0 1.7 %collective-permute-start = (bf16[2,33,8,128]{3,2,1,0:T(8,128)(2,1)}, bf16[2,33,8,128]{3,2,1,0:T(8,128)(2,1)S(1)}, u32[]{:S(2)}, u32[]{:S(2)}) collective-permute-start(bf16[2,33,8,128]{3,2,1,0:T(8,128)(2,1)} %bitcast.20), channel_id=1, source_target_pairs={{0,64},{64,0},{1,65},{65,1},{2,66},{66,2},{3,67},{67,3},{4,68},{68... | collective-permute-start | bytes 405512 | tf_op jit(solution)/shard_map/ppermute | solution.py:17
  0.0 1.7 %collective-permute-start.1 = (bf16[2,17,8,128]{3,2,1,0:T(8,128)(2,1)}, bf16[2,17,8,128]{3,2,1,0:T(8,128)(2,1)S(1)}, u32[]{:S(2)}, u32[]{:S(2)}) collective-permute-start(bf16[2,17,8,128]{3,2,1,0:T(8,128)(2,1)} %bitcast.22), channel_id=1, source_target_pairs={{0,64},{64,0},{1,65},{65,1},{2,66},{66,2},{3,67},{67,3},{4,68},{68... | collective-permute-start | bytes 208904 | tf_op jit(solution)/shard_map/ppermute | solution.py:17
  1.7 0.6 %copy-start.1 = (bf16[2,17,8,128]{3,2,1,0:T(8,128)(2,1)}, bf16[2,17,8,128]{3,2,1,0:T(8,128)(2,1)S(1)}, u32[]{:S(2)}) copy-start(bf16[2,17,8,128]{3,2,1,0:T(8,128)(2,1)S(1)} %collective-permute-done.1.yc_ref) | copy-start | bytes 208900
  1.7 0.7 %copy-start = (bf16[2,33,8,128]{3,2,1,0:T(8,128)(2,1)}, bf16[2,33,8,128]{3,2,1,0:T(8,128)(2,1)S(1)}, u32[]{:S(2)}) copy-start(bf16[2,33,8,128]{3,2,1,0:T(8,128)(2,1)S(1)} %collective-permute-done.xc_ref) | copy-start | bytes 405508

commit v3 on v0

v3 whole, which is shorter than its diff:
```python
import jax
import jax.numpy as jnp
from jax import lax
from jax.experimental import pallas as pl
from jax.experimental.pallas import tpu as pltpu
from jax.sharding import Mesh
from jax.sharding import PartitionSpec as P

TMPL = ("tmpl_0", "tmpl_1", "tmpl_2")
F32 = jnp.float32
BF = jnp.bfloat16
L = 128
VMEM = pl.BlockSpec(memory_space=pltpu.VMEM)
SMEM = pl.BlockSpec(memory_space=pltpu.SMEM)
ANY = pl.BlockSpec(memory_space=pl.ANY)
SMALL = pltpu.CompilerParams(vmem_limit_bytes=4 << 20)
LARGE = pltpu.CompilerParams(vmem_limit_bytes=24 << 20)


def iota(shape, axis):
    return lax.broadcasted_iota(jnp.int32, shape, axis)


def dot(a, b):
    return jnp.dot(a, b, preferred_element_type=F32)


def pack_kernel(part_ref, k_ref, x_ref, y_ref, op_ref, buf, sems):
    me = lax.axis_index(TMPL)
    loads = []
    for w in range(2):
        rows = slice(8 + 8 * w, 16 + 8 * w)
        loads.append(pltpu.make_async_copy(x_ref.at[w], buf.at[0:33, rows, :], sems.at[2 * w]))
        loads.append(pltpu.make_async_copy(y_ref.at[w], buf.at[33:50, rows, :], sems.at[2 * w + 1]))
    for load in loads:
        load.start()
    buf[50:64, 8:24, :] = jnp.zeros((14, 16, L), BF)
    wanted = jnp.concatenate(
        [
            (jnp.broadcast_to(part_ref[r : r + 1, :], (L, L)) == me * 16 + iota((L, L), 0) // 8).astype(BF)
            for r in range(8)
        ],
        axis=0,
    )
    group = (iota((64, L), 0) // 8 == iota((64, L), 1) // 16).astype(BF)
    hit = lax.dot_general(group, wanted, (((1,), (1,)), ((), ())), preferred_element_type=F32)
    same = iota((64, L), 0) % 8 == iota((64, L), 1) % 8
    pick = jnp.concatenate(
        [jnp.where(same, hit[:, r * L : (r + 1) * L], 0.0).astype(BF) for r in range(8)], axis=0
    )
    buf[:, 0:8, :] = dot(pick, k_ref[...]).reshape(64, 8, L).astype(BF)
    for load in loads:
        load.wait()
    store = pltpu.make_async_copy(buf, op_ref, sems.at[4])
    store.start()
    store.wait()


def held_column(owners_ref, w, row):
    held = jnp.where(owners_ref[w, 0] // 64 == row, 0, 1)
    return owners_ref[w, held] % 64


def extract_kernel(owners_ref, got_ref, out_ref, sems):
    row = lax.axis_index("trial")
    copies = []
    for w in range(2):
        block = got_ref.at[held_column(owners_ref, w, row), 8 + 8 * w : 16 + 8 * w, :]
        copies.append(pltpu.make_async_copy(block, out_ref.at[w], sems.at[w]))
    for copy in copies:
        copy.start()
    for copy in copies:
        copy.wait()


def repeat_kernel(owners_ref, own_ref, other_ref, out_ref):
    for w in range(2):
        crossed = owners_ref[w, 0] >= 64
        block = jnp.where(crossed, other_ref[w].astype(F32), own_ref[w].astype(F32)).astype(BF)
        out_ref[:, 8 * w : 8 * w + 8, :] = jnp.broadcast_to(block[None], (64, 8, L))


def prepare_kernel(part_ref, k_ref, got_ref, rev_ref, h, sems):
    me = lax.axis_index(TMPL)
    copies = []
    for s in range(16):
        source = jnp.maximum(part_ref[me * 16 + s], 0) // 16
        copies.append(pltpu.make_async_copy(got_ref.at[source, 0:8, :], h.at[s], sems.at[s]))
    for copy in copies:
        copy.start()
    flip = (iota((L, L), 0) == (L - iota((L, L), 1)) % L).astype(BF)
    rev_ref[0] = dot(k_ref[...], flip)
    for copy in copies:
        copy.wait()
    rev_ref[1] = dot(h[...].astype(F32).reshape(L, L).astype(BF), flip)


def correlate_kernel(
    counts_ref, whole_ref, rev_ref, out_ref, whole, flat, y64, lx, ly, ra, rb, scr, obuf, sems
):
    me = lax.axis_index(TMPL)
    fetch = pltpu.make_async_copy(whole_ref, whole, sems.at[0])
    fetch.start()
    tri = iota((L, L), 0) >= iota((L, L), 1)
    tri_half = iota((L, L), 0) >= iota((L, L), 1) % 64
    left = iota((L, L), 1) < 64
    zero = jnp.zeros((L, L), F32)
    live_n = counts_ref[me]

    def circulant(kind, row, shift):
        v = jnp.broadcast_to(rev_ref[kind, pl.ds(row, 1), :], (L, L))
        return pltpu.roll(v, shift, 1, stride=1, stride_axis=0)

    def bands(cs, mask):
        first = [jnp.where(mask, cs[0], zero)]
        return first + [jnp.where(mask, cs[q], cs[q - 1]) for q in (1, 2, 3)] + [jnp.where(mask, zero, cs[3])]

    def put(dst, c, side, tiles):
        for q in range(5):
            dst[(5 * c + q) * L : (5 * c + q + 1) * L, side * L : (side + 1) * L] = tiles[q].astype(BF)

    def build(group, dst):
        for k in range(4):
            for c in range(2):
                row = (4 * group + k) * 8 + c
                put(dst.at[k // 2], c, k % 2, bands([circulant(0, row + 2 * q, 0) for q in range(4)], tri))
        for k in range(2):
            for c in range(2):
                row = (4 * group + 2 * k) * 8 + c
                both = [
                    jnp.where(left, circulant(1, row + 2 * q, 0), circulant(1, row + 8 + 2 * q, 64))
                    for q in range(4)
                ]
                put(dst.at[2], c, k, bands(both, tri_half))

    dup = (iota((L, 2 * L), 0) == (iota((L, 2 * L), 1) // L) * 64 + (iota((L, 2 * L), 1) % L) // 2).astype(BF)

    def power(rows, taps):
        z = dot(rows[...], taps[...])
        return z[:256] * z[:256] + z[256:] * z[256:]

    def work(group, src):
        plane = power(ly, src.at[2]).astype(BF)
        for k in range(2):
            wide = dot(plane[:, k * L : (k + 1) * L], dup)
            total = power(lx, src.at[k]) + wide
            for j in range(2):
                t = 4 * group + 2 * k + j
                scr[pl.ds(t, 256, stride=16), :] = jnp.where(t < live_n, total[:, j * L : (j + 1) * L], 0.0)

    build(0, ra)
    fetch.wait()
    lane = iota((68, L), 1)
    for w in range(2):
        flat[w] = whole[:, 8 * w : 8 * w + 8, :].astype(F32).reshape(512, L)
        top, low = slice(w * L, (w + 1) * L), slice(256 + w * L, 256 + (w + 1) * L)
        for c in range(2):
            even = flat[w, pl.ds(264 + c, 68, stride=2), :]
            after = flat[w, pl.ds(266 + c, 68, stride=2), :]
            y64[pl.ds(0, 68, stride=2), :] = even
            y64[pl.ds(1, 68, stride=2), :] = jnp.where(lane < 64, pltpu.roll(even, 64, 1), pltpu.roll(after, 64, 1))
            for q in range(5):
                here = slice((5 * c + q) * L, (5 * c + q + 1) * L)
                there = slice((5 - 5 * c + q) * L, (6 - 5 * c + q) * L)
                for dst, v in (
                    (lx, flat[w, pl.ds(2 * q + c, L, stride=2), :]),
                    (ly, y64[2 * q : 2 * q + L, :]),
                ):
                    dst[top, here] = (v if c == 0 else -v).astype(BF)
                    dst[low, there] = v.astype(BF)

    def step(i, carry):
        build(2 * i + 1, rb)
        work(2 * i, ra)
        build(jnp.minimum(2 * i + 2, 3), ra)
        work(2 * i + 1, rb)
        return carry

    lax.fori_loop(0, 2, step, 0)
    stores = []
    for w in range(2):

        def merge(a, carry):
            for u in range(8):
                at = (w * L + 8 * a + u) * 16
                cols = pl.ds(pl.multiple_of((8 * a + u) * L, L), L)
                obuf[w, :, cols] = scr[pl.ds(pl.multiple_of(at, 16), 16), :].astype(BF)
            return carry

        lax.fori_loop(0, 16, merge, 0)
        stores.append(pltpu.make_async_copy(obuf.at[w], out_ref.at[w], sems.at[1 + w]))
        stores[-1].start()
    for store in stores:
        store.wait()


def body(spectra, half_spectra, kernels, owners, counts, partners):
    x = spectra.reshape(2, 2, 33, 4, L).transpose(0, 2, 3, 1, 4).reshape(2, 33, 8, L)
    y = half_spectra.reshape(2, 2, 17, 4, L).transpose(0, 2, 3, 1, 4).reshape(2, 17, 8, L)
    k = kernels.reshape(16, 2, 4, L).transpose(0, 2, 1, 3).reshape(L, L)
    dma = pltpu.SemaphoreType.DMA
    sent = pl.pallas_call(
        pack_kernel,
        out_shape=jax.ShapeDtypeStruct((64, 24, L), BF),
        in_specs=[VMEM, VMEM, ANY, ANY],
        out_specs=ANY,
        scratch_shapes=[pltpu.VMEM((64, 24, L), BF), dma((5,))],
        name="pack",
    )(partners.reshape(8, L), k, x, y)
    got = lax.all_to_all(sent, TMPL, 0, 0, tiled=True)
    own = pl.pallas_call(
        extract_kernel,
        out_shape=jax.ShapeDtypeStruct((2, 8, L), BF),
        in_specs=[SMEM, ANY],
        out_specs=VMEM,
        scratch_shapes=[dma((2,))],
        compiler_params=SMALL,
        name="extract",
    )(owners, got)
    other = lax.ppermute(own, "trial", [(0, 1), (1, 0)])
    repeated = pl.pallas_call(
        repeat_kernel,
        out_shape=jax.ShapeDtypeStruct((64, 16, L), BF),
        in_specs=[SMEM, VMEM, VMEM],
        out_specs=VMEM,
        compiler_params=SMALL,
        name="repeat",
    )(owners, own, other)
    rev = pl.pallas_call(
        prepare_kernel,
        out_shape=jax.ShapeDtypeStruct((2, L, L), F32),
        in_specs=[SMEM, VMEM, ANY],
        out_specs=VMEM,
        scratch_shapes=[pltpu.VMEM((16, 8, L), BF), dma((16,))],
        cost_estimate=pl.CostEstimate(flops=10**7, bytes_accessed=10**6, transcendentals=0),
        compiler_params=SMALL,
        name="prepare",
    )(partners, k, got)
    whole = lax.all_to_all(repeated, TMPL, 0, 0, tiled=True)
    out = pl.pallas_call(
        correlate_kernel,
        out_shape=jax.ShapeDtypeStruct((2, 16, 16384), BF),
        in_specs=[SMEM, ANY, VMEM],
        out_specs=ANY,
        scratch_shapes=[
            pltpu.VMEM((64, 16, L), BF),
            pltpu.VMEM((2, 512, L), F32),
            pltpu.VMEM((136, L), F32),
            pltpu.VMEM((512, 1280), BF),
            pltpu.VMEM((512, 1280), BF),
            pltpu.VMEM((3, 1280, 256), BF),
            pltpu.VMEM((3, 1280, 256), BF),
            pltpu.VMEM((4096, L), F32),
            pltpu.VMEM((2, 16, 16384), BF),
            dma((3,)),
        ],
        compiler_params=LARGE,
        name="correlate",
    )(counts, whole, rev)
    return out[:, None]


def solution(mesh):
    finer = Mesh(
        mesh.devices.reshape(mesh.shape["trial"], 4, 4, 4), ("trial", "tmpl_0", "tmpl_1", "tmpl_2")
    )
    in_specs = (
        P(None, "trial", TMPL, None, None),
        P(None, "trial", TMPL, None, None),
        P(TMPL, None, None),
        P(),
        P(),
        P(),
    )
    out_specs = P(None, "trial", TMPL, None)
    return jax.shard_map(body, mesh=finer, in_specs=in_specs, out_specs=out_specs, check_vma=False)
```

time: 1250 us -> 54.9 us (0.04)
  local copies, waits for them, and re-layouts: 1010 us -> 0.02 us
  waiting for transfers between devices: 129 us -> 9.6 us
  other arithmetic: 45.8 us -> 0 us
  matrix products: 23 us -> 0 us
  blocking collectives: 0 us -> 22.9 us
  between operations: 17.3 us -> 0.07 us
  Pallas kernels: 0 us -> 15 us
    reshape x51 -> x0, local copies, waits for them, and re-layouts: 354 us -> none  [the longest x48 353 us: hankel_rows(): repeated[:, :tap_count * (length + 1)].reshape(2, tap_count, length + 1)]
    while x178 -> x0, local copies, waits for them, and re-layouts: 323 us -> none
    slice x152 -> x0, local copies, waits for them, and re-layouts: 289 us -> none  [the longest x48 209 us: hankel_rows(): repeated[:, :tap_count * (length + 1)].reshape(2, tap_count, length + 1)]
    psum x3 -> x0, waiting for transfers between devices: 128 us -> none  [spread(): x = lax.psum(x, axis)]
    dynamic_update_slice x48 -> x0, other arithmetic: 25.9 us -> none  [add_block(): return lax.dynamic_update_slice_in_dim(result, values, first_bin, 1)]
    dot_general x51 -> x0, matrix products: 23 us -> none  [the longest x48 22.3 us: power_rows(): product = jnp.dot(weights, stacked, preferred_element_type=jnp.float32)]
    all_to_all x0 -> x1, blocking collectives: none -> 22.9 us  [body(): got = lax.all_to_all(sent, TMPL, 0, 0, tiled=True)]
    dynamic_slice x50 -> x0, local copies, waits for them, and re-layouts: 17.8 us -> none  [the longest x48 17 us: add_block(): lax.dynamic_slice_in_dim(signal, first_bin, block_rows + tap_count, 1)]
  transfers between devices with their start and end apart: 6 -> 2, of which waited for: 4 -> 2; matrix products, arithmetic and copies ran while one was open for 1% -> 0% of each run, Pallas kernels for 0% -> 2%
where the time goes in v3:
time: 54.9 us; the launch traced here: 54.4 us
  blocking collectives  22.9 us (42%)
  Pallas kernels  15 us (27%)
  waiting for transfers between devices  9.6 us (17%)
  starting transfers between devices  6.8 us (12%)
    all_to_all x1, blocking collectives, body(): got = lax.all_to_all(sent, TMPL, 0, 0, tiled=True)  22.9 us
    pallas_call x1, Pallas kernels, body(): pl.pallas_call(correlate_kernel, out_shape=jax.ShapeDtypeStruct((2, 16, 1...  9.44 us
    all_to_all x1, waiting for transfers between devices, body(): whole = lax.all_to_all(repeated, TMPL, 0, 0, tiled=True)  8.77 us
    all_to_all x1, starting transfers between devices, body(): whole = lax.all_to_all(repeated, TMPL, 0, 0, tiled=True)  4.76 us
    pallas_call x1, Pallas kernels, body(): pl.pallas_call(pack_kernel, out_shape=jax.ShapeDtypeStruct((64, 24, L), B...  2.51 us
    ppermute x1, starting transfers between devices, body(): other = lax.ppermute(own, 'trial', [(0, 1), (1, 0)])  2.04 us
    pallas_call x1, Pallas kernels, body(): pl.pallas_call(repeat_kernel, out_shape=jax.ShapeDtypeStruct((64, 16, L),...  1.29 us
    pallas_call x1, Pallas kernels, body(): pl.pallas_call(prepare_kernel, out_shape=jax.ShapeDtypeStruct((2, L, L),...  1.17 us
  transfers between devices with their start and end apart: 2, of which 2 were waited for; matrix products, arithmetic and copies ran while one was open for 0% of the time, Pallas kernels for 2%

profile of v3, /device:TPU:1, one launch (start us, length us, event | category | flops | bytes accessed | tf_op | source)
XLA Modules:
  0.0 54.4 jit_solution(3097242394133040855)
XLA Ops:
  0.0 2.5 %pack.1 = bf16[64,24,128]{2,1,0:T(8,128)(2,1)} custom-call(s32[8,128]{1,0:T(8,128)} %bitcast.21, bf16[128,128]{1,0:T(8,128)(2,1)} %bitcast.19, bf16[2,33,8,128]{3,2,1,0:T(8,128)(2,1)} %bitcast.22, bf16[2,17,8,128]{3,2,1,0:T(8,128)(2,1)} %bitcast.23), custom_call_target="tpu_custom_call" | custom-call | tf_op jit(solution)/shard_map/pack/pallas_call | solution.py:202
  2.5 0.0 copy-start.2
  2.5 22.9 %all_to_all.10.got_ref = bf16[64,24,128]{2,1,0:T(8,128)(2,1)S(1)} all-to-all(bf16[64,24,128]{2,1,0:T(8,128)(2,1)} %pack.1), channel_id=1, replica_groups=mesh['trial'=2,'tmpl_0'=4,'tmpl_1'=4,'tmpl_2'=4] {'tmpl_0','tmpl_1','tmp..., dimensions={0} | all-to-all | bytes 786432 | tf_op jit(solution)/shard_map/all_to_all | solution.py:210
  25.4 0.0 copy-done.2
  25.4 0.6 %extract.1.own_ref = bf16[2,8,128]{2,1,0:T(8,128)(2,1)S(1)} custom-call(s32[2,2]{1,0:T(2,128)S(1)} %copy-done.2, bf16[64,24,128]{2,1,0:T(8,128)(2,1)S(1)} %all_to_all.10.got_ref), custom_call_target="tpu_custom_call" | custom-call | tf_op jit(solution)/shard_map/extract/pallas_call | solution.py:211
  26.0 2.0 %collective-permute-start = (bf16[2,8,128]{2,1,0:T(8,128)(2,1)S(1)}, bf16[2,8,128]{2,1,0:T(8,128)(2,1)S(1)}, u32[]{:S(2)}, u32[]{:S(2)}) collective-permute-start(bf16[2,8,128]{2,1,0:T(8,128)(2,1)S(1)} %extract.1.own_ref), channel_id=1, source_target_pairs={{0,64},{64,0},{1,65},{65,1},{2,66},{66,2},{3,67},{67,3},{4,68},{68... | collective-permute-start | bytes 12296 | tf_op jit(solution)/shard_map/ppermute | solution.py:220
  28.1 0.8 %collective-permute-done.other_ref = bf16[2,8,128]{2,1,0:T(8,128)(2,1)S(1)} collective-permute-done((bf16[2,8,128]{2,1,0:T(8,128)(2,1)S(1)}, bf16[2,8,128]{2,1,0:T(8,128)(2,1)S(1)}, u32[]{:S(2)}, u32[]{:S(2)}) %collective-permute-start) | collective-permute-done | bytes 4128 | tf_op jit(solution)/shard_map/ppermute | solution.py:220
  28.9 1.3 %repeat.1 = bf16[64,16,128]{2,1,0:T(8,128)(2,1)} custom-call(s32[2,2]{1,0:T(2,128)S(1)} %copy-done.2, bf16[2,8,128]{2,1,0:T(8,128)(2,1)S(1)} %extract.1.own_ref, bf16[2,8,128]{2,1,0:T(8,128)(2,1)S(1)} %collective-permute-done.other_ref), custom_call_target="tpu_custom_call" | custom-call | tf_op jit(solution)/shard_map/repeat/pallas_call | solution.py:221
  30.2 0.0 copy-start
  30.2 0.0 copy-start.1
  30.2 4.8 %all-to-all-start.1 = ((bf16[64,16,128]{2,1,0:T(8,128)(2,1)}), bf16[64,16,128]{2,1,0:T(8,128)(2,1)S(1)}, u32[]{:S(2)}, u32[]{:S(2)}) async-start(bf16[64,16,128]{2,1,0:T(8,128)(2,1)} %repeat.1), calls=%async_computation.1 | async-start | bytes 524288 | tf_op jit(solution)/shard_map/all_to_all | solution.py:239
  34.9 0.0 copy-done
  34.9 0.0 copy-done.1
  35.0 0.0 copy-start.3
  35.0 1.2 %prepare.1.rev_ref = f32[2,128,128]{2,1,0:T(8,128)S(1)} custom-call(s32[1024]{0:T(1024)S(1)} %copy-done.1, bf16[128,128]{1,0:T(8,128)(2,1)S(1)} %bitcast.20, bf16[64,24,128]{2,1,0:T(8,128)(2,1)S(1)} %all_to_all.10.got_ref), custom_call_target="tpu_custom_call" | custom-call | flops 10000000 | bytes 1000000 | tf_op jit(solution)/shard_map/prepare/pallas_call | solution.py:229
  36.1 8.8 %all-to-all-done.1.whole_ref = bf16[64,16,128]{2,1,0:T(8,128)(2,1)S(1)} async-done(((bf16[64,16,128]{2,1,0:T(8,128)(2,1)}), bf16[64,16,128]{2,1,0:T(8,128)(2,1)S(1)}, u32[]{:S(2)}, u32[]{:S(2)}) %all-to-all-start.1) | async-done | bytes 262176 | tf_op jit(solution)/shard_map/all_to_all | solution.py:239
  44.9 0.0 copy-done.3
  44.9 9.4 %correlate.1 = bf16[2,16,16384]{2,1,0:T(8,128)(2,1)} custom-call(s32[64]{0:T(128)S(1)} %copy-done.3, bf16[64,16,128]{2,1,0:T(8,128)(2,1)S(1)} %all-to-all-done.1.whole_ref, f32[2,128,128]{2,1,0:T(8,128)S(1)} %prepare.1.rev_ref), custom_call_target="tpu_custom_call" | custom-call | tf_op jit(solution)/shard_map/correlate/pallas_call | solution.py:240
Async XLA Ops:
  2.5 22.9 %copy-start.2 = (s32[2,2]{1,0:T(2,128)S(1)}, s32[2,2]{1,0:T(2,128)}, u32[]{:S(2)}) copy-start(s32[2,2]{1,0:T(2,128)} %owners_ref.3) | copy-start | bytes 52
  26.0 2.9 %collective-permute-start = (bf16[2,8,128]{2,1,0:T(8,128)(2,1)S(1)}, bf16[2,8,128]{2,1,0:T(8,128)(2,1)S(1)}, u32[]{:S(2)}, u32[]{:S(2)}) collective-permute-start(bf16[2,8,128]{2,1,0:T(8,128)(2,1)S(1)} %extract.1.own_ref), channel_id=1, source_target_pairs={{0,64},{64,0},{1,65},{65,1},{2,66},{66,2},{3,67},{67,3},{4,68},{68... | collective-permute-start | bytes 12296 | tf_op jit(solution)/shard_map/ppermute | solution.py:220
  30.2 4.8 %copy-start = (bf16[16,2,512]{2,1,0:T(2,128)(2,1)S(1)}, bf16[16,2,512]{2,1,0:T(2,128)(2,1)}, u32[]{:S(2)}) copy-start(bf16[16,2,512]{2,1,0:T(2,128)(2,1)} %param.8) | copy-start | bytes 98308
  30.2 4.8 %copy-start.1 = (s32[1024]{0:T(1024)S(1)}, s32[1024]{0:T(1024)}, u32[]{:S(2)}) copy-start(s32[1024]{0:T(1024)} %part_ref.1) | copy-start | bytes 12292
  30.2 14.7 %all-to-all-start.1 = ((bf16[64,16,128]{2,1,0:T(8,128)(2,1)}), bf16[64,16,128]{2,1,0:T(8,128)(2,1)S(1)}, u32[]{:S(2)}, u32[]{:S(2)}) async-start(bf16[64,16,128]{2,1,0:T(8,128)(2,1)} %repeat.1), calls=%async_computation.1 | async-start | bytes 524288 | tf_op jit(solution)/shard_map/all_to_all | solution.py:239
  35.0 10.0 %copy-start.3 = (s32[64]{0:T(128)S(1)}, s32[64]{0:T(128)}, u32[]{:S(2)}) copy-start(s32[64]{0:T(128)} %counts_ref.1) | copy-start | bytes 772

commit v4 on v3

--- a/solution.py
+++ b/solution.py
@@ -96,11 +96,9 @@
 
 
 def correlate_kernel(
-    counts_ref, whole_ref, rev_ref, out_ref, whole, flat, y64, lx, ly, ra, rb, scr, obuf, sems
+    counts_ref, whole, rev_ref, out_ref, flat, y64, lx, ly, ra, rb, scr, obuf, sems
 ):
     me = lax.axis_index(TMPL)
-    fetch = pltpu.make_async_copy(whole_ref, whole, sems.at[0])
-    fetch.start()
     tri = iota((L, L), 0) >= iota((L, L), 1)
     tri_half = iota((L, L), 0) >= iota((L, L), 1) % 64
     left = iota((L, L), 1) < 64
@@ -136,8 +134,9 @@
     dup = (iota((L, 2 * L), 0) == (iota((L, 2 * L), 1) // L) * 64 + (iota((L, 2 * L), 1) % L) // 2).astype(BF)
 
     def power(rows, taps):
-        z = dot(rows[...], taps[...])
-        return z[:256] * z[:256] + z[256:] * z[256:]
+        re = dot(rows[0:256, :], taps[...])
+        im = dot(rows[256:512, :], taps[...])
+        return re * re + im * im
 
     def work(group, src):
         plane = power(ly, src.at[2]).astype(BF)
@@ -149,7 +148,6 @@
                 scr[pl.ds(t, 256, stride=16), :] = jnp.where(t < live_n, total[:, j * L : (j + 1) * L], 0.0)
 
     build(0, ra)
-    fetch.wait()
     lane = iota((68, L), 1)
     for w in range(2):
         flat[w] = whole[:, 8 * w : 8 * w + 8, :].astype(F32).reshape(512, L)
@@ -169,26 +167,25 @@
                     dst[top, here] = (v if c == 0 else -v).astype(BF)
                     dst[low, there] = v.astype(BF)
 
-    def step(i, carry):
-        build(2 * i + 1, rb)
-        work(2 * i, ra)
-        build(jnp.minimum(2 * i + 2, 3), ra)
-        work(2 * i + 1, rb)
-        return carry
-
-    lax.fori_loop(0, 2, step, 0)
+    for group in range(4):
+        if group < 3:
+            build(group + 1, (ra, rb)[(group + 1) % 2])
+        work(group, (ra, rb)[group % 2])
     stores = []
-    for w in range(2):
+    for part in range(8):
+        w, first = part // 4, part % 4 * 32
 
         def merge(a, carry):
             for u in range(8):
-                at = (w * L + 8 * a + u) * 16
-                cols = pl.ds(pl.multiple_of((8 * a + u) * L, L), L)
-                obuf[w, :, cols] = scr[pl.ds(pl.multiple_of(at, 16), 16), :].astype(BF)
+                at = first + 8 * a + u
+                cols = pl.ds(pl.multiple_of(at * L, L), L)
+                rows = pl.ds(pl.multiple_of((w * L + at) * 16, 16), 16)
+                obuf[w, :, cols] = scr[rows, :].astype(BF)
             return carry
 
-        lax.fori_loop(0, 16, merge, 0)
-        stores.append(pltpu.make_async_copy(obuf.at[w], out_ref.at[w], sems.at[1 + w]))
+        lax.fori_loop(0, 4, merge, 0, unroll=True)
+        cols = slice(first * L, (first + 32) * L)
+        stores.append(pltpu.make_async_copy(obuf.at[w, :, cols], out_ref.at[w, :, cols], sems.at[part]))
         stores[-1].start()
     for store in stores:
         store.wait()
@@ -240,10 +237,9 @@
     out = pl.pallas_call(
         correlate_kernel,
         out_shape=jax.ShapeDtypeStruct((2, 16, 16384), BF),
-        in_specs=[SMEM, ANY, VMEM],
+        in_specs=[SMEM, VMEM, VMEM],
         out_specs=ANY,
         scratch_shapes=[
-            pltpu.VMEM((64, 16, L), BF),
             pltpu.VMEM((2, 512, L), F32),
             pltpu.VMEM((136, L), F32),
             pltpu.VMEM((512, 1280), BF),
@@ -252,7 +248,7 @@
             pltpu.VMEM((3, 1280, 256), BF),
             pltpu.VMEM((4096, L), F32),
             pltpu.VMEM((2, 16, 16384), BF),
-            dma((3,)),
+            dma((8,)),
         ],
         compiler_params=LARGE,
         name="correlate",

time: 54.9 us -> 52.8 us (0.962)
  Pallas kernels: 15 us -> 12.9 us
    pallas_call x1, Pallas kernels: 9.44 us -> 7.33 us  [body(): pl.pallas_call(correlate_kernel, out_shape=jax.ShapeDtypeStruct((2, 16, 1...]
where the time goes in v4:
time: 52.8 us; the launch traced here: 52.3 us
  blocking collectives  22.9 us (43%)
  Pallas kernels  12.9 us (24%)
  waiting for transfers between devices  9.6 us (18%)
  starting transfers between devices  6.8 us (13%)
    all_to_all x1, blocking collectives, body(): got = lax.all_to_all(sent, TMPL, 0, 0, tiled=True)  22.9 us
    all_to_all x1, waiting for transfers between devices, body(): whole = lax.all_to_all(repeated, TMPL, 0, 0, tiled=True)  8.77 us
    pallas_call x1, Pallas kernels, body(): pl.pallas_call(correlate_kernel, out_shape=jax.ShapeDtypeStruct((2, 16, 1...  7.33 us
    all_to_all x1, starting transfers between devices, body(): whole = lax.all_to_all(repeated, TMPL, 0, 0, tiled=True)  4.76 us
    pallas_call x1, Pallas kernels, body(): pl.pallas_call(pack_kernel, out_shape=jax.ShapeDtypeStruct((64, 24, L), B...  2.51 us
    ppermute x1, starting transfers between devices, body(): other = lax.ppermute(own, 'trial', [(0, 1), (1, 0)])  2.04 us
    pallas_call x1, Pallas kernels, body(): pl.pallas_call(repeat_kernel, out_shape=jax.ShapeDtypeStruct((64, 16, L),...  1.29 us
    pallas_call x1, Pallas kernels, body(): pl.pallas_call(prepare_kernel, out_shape=jax.ShapeDtypeStruct((2, L, L),...  1.17 us
  transfers between devices with their start and end apart: 2, of which 2 were waited for; matrix products, arithmetic and copies ran while one was open for 0% of the time, Pallas kernels for 2%

profile of v4, /device:TPU:1, one launch (start us, length us, event | category | flops | bytes accessed | tf_op | source)
XLA Modules:
  0.0 52.3 jit_solution(7453715018004926664)
XLA Ops:
  0.0 2.5 %pack.1 = bf16[64,24,128]{2,1,0:T(8,128)(2,1)} custom-call(s32[8,128]{1,0:T(8,128)} %bitcast.21, bf16[128,128]{1,0:T(8,128)(2,1)} %bitcast.19, bf16[2,33,8,128]{3,2,1,0:T(8,128)(2,1)} %bitcast.22, bf16[2,17,8,128]{3,2,1,0:T(8,128)(2,1)} %bitcast.23), custom_call_target="tpu_custom_call" | custom-call | tf_op jit(solution)/shard_map/pack/pallas_call | solution.py:199
  2.5 0.0 copy-start.2
  2.5 22.9 %all_to_all.10.got_ref = bf16[64,24,128]{2,1,0:T(8,128)(2,1)S(1)} all-to-all(bf16[64,24,128]{2,1,0:T(8,128)(2,1)} %pack.1), channel_id=1, replica_groups=mesh['trial'=2,'tmpl_0'=4,'tmpl_1'=4,'tmpl_2'=4] {'tmpl_0','tmpl_1','tmp..., dimensions={0} | all-to-all | bytes 786432 | tf_op jit(solution)/shard_map/all_to_all | solution.py:207
  25.4 0.0 copy-done.2
  25.4 0.6 %extract.1.own_ref = bf16[2,8,128]{2,1,0:T(8,128)(2,1)S(1)} custom-call(s32[2,2]{1,0:T(2,128)S(1)} %copy-done.2, bf16[64,24,128]{2,1,0:T(8,128)(2,1)S(1)} %all_to_all.10.got_ref), custom_call_target="tpu_custom_call" | custom-call | tf_op jit(solution)/shard_map/extract/pallas_call | solution.py:208
  26.0 2.0 %collective-permute-start = (bf16[2,8,128]{2,1,0:T(8,128)(2,1)S(1)}, bf16[2,8,128]{2,1,0:T(8,128)(2,1)S(1)}, u32[]{:S(2)}, u32[]{:S(2)}) collective-permute-start(bf16[2,8,128]{2,1,0:T(8,128)(2,1)S(1)} %extract.1.own_ref), channel_id=1, source_target_pairs={{0,64},{64,0},{1,65},{65,1},{2,66},{66,2},{3,67},{67,3},{4,68},{68... | collective-permute-start | bytes 12296 | tf_op jit(solution)/shard_map/ppermute | solution.py:217
  28.1 0.8 %collective-permute-done.other_ref = bf16[2,8,128]{2,1,0:T(8,128)(2,1)S(1)} collective-permute-done((bf16[2,8,128]{2,1,0:T(8,128)(2,1)S(1)}, bf16[2,8,128]{2,1,0:T(8,128)(2,1)S(1)}, u32[]{:S(2)}, u32[]{:S(2)}) %collective-permute-start) | collective-permute-done | bytes 4128 | tf_op jit(solution)/shard_map/ppermute | solution.py:217
  28.9 1.3 %repeat.1 = bf16[64,16,128]{2,1,0:T(8,128)(2,1)} custom-call(s32[2,2]{1,0:T(2,128)S(1)} %copy-done.2, bf16[2,8,128]{2,1,0:T(8,128)(2,1)S(1)} %extract.1.own_ref, bf16[2,8,128]{2,1,0:T(8,128)(2,1)S(1)} %collective-permute-done.other_ref), custom_call_target="tpu_custom_call" | custom-call | tf_op jit(solution)/shard_map/repeat/pallas_call | solution.py:218
  30.2 0.0 copy-start
  30.2 0.0 copy-start.1
  30.2 4.8 %all-to-all-start.1 = ((bf16[64,16,128]{2,1,0:T(8,128)(2,1)}), bf16[64,16,128]{2,1,0:T(8,128)(2,1)S(1)}, u32[]{:S(2)}, u32[]{:S(2)}) async-start(bf16[64,16,128]{2,1,0:T(8,128)(2,1)} %repeat.1), calls=%async_computation.1 | async-start | bytes 524288 | tf_op jit(solution)/shard_map/all_to_all | solution.py:236
  34.9 0.0 copy-done
  34.9 0.0 copy-done.1
  35.0 0.0 copy-start.3
  35.0 1.2 %prepare.1.rev_ref = f32[2,128,128]{2,1,0:T(8,128)S(1)} custom-call(s32[1024]{0:T(1024)S(1)} %copy-done.1, bf16[128,128]{1,0:T(8,128)(2,1)S(1)} %bitcast.20, bf16[64,24,128]{2,1,0:T(8,128)(2,1)S(1)} %all_to_all.10.got_ref), custom_call_target="tpu_custom_call" | custom-call | flops 10000000 | bytes 1000000 | tf_op jit(solution)/shard_map/prepare/pallas_call | solution.py:226
  36.1 8.8 %all-to-all-done.1.whole = bf16[64,16,128]{2,1,0:T(8,128)(2,1)S(1)} async-done(((bf16[64,16,128]{2,1,0:T(8,128)(2,1)}), bf16[64,16,128]{2,1,0:T(8,128)(2,1)S(1)}, u32[]{:S(2)}, u32[]{:S(2)}) %all-to-all-start.1) | async-done | bytes 262176 | tf_op jit(solution)/shard_map/all_to_all | solution.py:236
  44.9 0.0 copy-done.3
  44.9 7.3 %correlate.1 = bf16[2,16,16384]{2,1,0:T(8,128)(2,1)} custom-call(s32[64]{0:T(128)S(1)} %copy-done.3, bf16[64,16,128]{2,1,0:T(8,128)(2,1)S(1)} %all-to-all-done.1.whole, f32[2,128,128]{2,1,0:T(8,128)S(1)} %prepare.1.rev_ref), custom_call_target="tpu_custom_call" | custom-call | tf_op jit(solution)/shard_map/correlate/pallas_call | solution.py:237
Async XLA Ops:
  2.5 22.9 %copy-start.2 = (s32[2,2]{1,0:T(2,128)S(1)}, s32[2,2]{1,0:T(2,128)}, u32[]{:S(2)}) copy-start(s32[2,2]{1,0:T(2,128)} %owners_ref.3) | copy-start | bytes 52
  26.0 2.9 %collective-permute-start = (bf16[2,8,128]{2,1,0:T(8,128)(2,1)S(1)}, bf16[2,8,128]{2,1,0:T(8,128)(2,1)S(1)}, u32[]{:S(2)}, u32[]{:S(2)}) collective-permute-start(bf16[2,8,128]{2,1,0:T(8,128)(2,1)S(1)} %extract.1.own_ref), channel_id=1, source_target_pairs={{0,64},{64,0},{1,65},{65,1},{2,66},{66,2},{3,67},{67,3},{4,68},{68... | collective-permute-start | bytes 12296 | tf_op jit(solution)/shard_map/ppermute | solution.py:217
  30.2 4.8 %copy-start = (bf16[16,2,512]{2,1,0:T(2,128)(2,1)S(1)}, bf16[16,2,512]{2,1,0:T(2,128)(2,1)}, u32[]{:S(2)}) copy-start(bf16[16,2,512]{2,1,0:T(2,128)(2,1)} %param.8) | copy-start | bytes 98308
  30.2 4.8 %copy-start.1 = (s32[1024]{0:T(1024)S(1)}, s32[1024]{0:T(1024)}, u32[]{:S(2)}) copy-start(s32[1024]{0:T(1024)} %part_ref.1) | copy-start | bytes 12292
  30.2 14.7 %all-to-all-start.1 = ((bf16[64,16,128]{2,1,0:T(8,128)(2,1)}), bf16[64,16,128]{2,1,0:T(8,128)(2,1)S(1)}, u32[]{:S(2)}, u32[]{:S(2)}) async-start(bf16[64,16,128]{2,1,0:T(8,128)(2,1)} %repeat.1), calls=%async_computation.1 | async-start | bytes 524288 | tf_op jit(solution)/shard_map/all_to_all | solution.py:236
  35.0 10.0 %copy-start.3 = (s32[64]{0:T(128)S(1)}, s32[64]{0:T(128)}, u32[]{:S(2)}) copy-start(s32[64]{0:T(128)} %counts_ref.1) | copy-start | bytes 772

commit v5 on v4

--- a/solution.py
+++ b/solution.py
@@ -25,8 +25,14 @@
     return jnp.dot(a, b, preferred_element_type=F32)
 
 
-def pack_kernel(part_ref, k_ref, x_ref, y_ref, op_ref, buf, sems):
+def pack_kernel(part_hbm, k_hbm, x_ref, y_ref, op_ref, part_ref, k_ref, buf, sems):
     me = lax.axis_index(TMPL)
+    tables = (
+        pltpu.make_async_copy(part_hbm, part_ref, sems.at[5]),
+        pltpu.make_async_copy(k_hbm, k_ref, sems.at[6]),
+    )
+    for table in tables:
+        table.start()
     loads = []
     for w in range(2):
         rows = slice(8 + 8 * w, 16 + 8 * w)
@@ -35,6 +41,10 @@
     for load in loads:
         load.start()
     buf[50:64, 8:24, :] = jnp.zeros((14, 16, L), BF)
+    group = (iota((64, L), 0) // 8 == iota((64, L), 1) // 16).astype(BF)
+    same = iota((64, L), 0) % 8 == iota((64, L), 1) % 8
+    for table in tables:
+        table.wait()
     wanted = jnp.concatenate(
         [
             (jnp.broadcast_to(part_ref[r : r + 1, :], (L, L)) == me * 16 + iota((L, L), 0) // 8).astype(BF)
@@ -42,9 +52,7 @@
         ],
         axis=0,
     )
-    group = (iota((64, L), 0) // 8 == iota((64, L), 1) // 16).astype(BF)
     hit = lax.dot_general(group, wanted, (((1,), (1,)), ((), ())), preferred_element_type=F32)
-    same = iota((64, L), 0) % 8 == iota((64, L), 1) % 8
     pick = jnp.concatenate(
         [jnp.where(same, hit[:, r * L : (r + 1) * L], 0.0).astype(BF) for r in range(8)], axis=0
     )
@@ -56,28 +64,13 @@
     store.wait()
 
 
-def held_column(owners_ref, w, row):
-    held = jnp.where(owners_ref[w, 0] // 64 == row, 0, 1)
-    return owners_ref[w, held] % 64
-
-
-def extract_kernel(owners_ref, got_ref, out_ref, sems):
+def relay_kernel(owners_ref, got_ref, out_ref):
     row = lax.axis_index("trial")
-    copies = []
-    for w in range(2):
-        block = got_ref.at[held_column(owners_ref, w, row), 8 + 8 * w : 16 + 8 * w, :]
-        copies.append(pltpu.make_async_copy(block, out_ref.at[w], sems.at[w]))
-    for copy in copies:
-        copy.start()
-    for copy in copies:
-        copy.wait()
-
-
-def repeat_kernel(owners_ref, own_ref, other_ref, out_ref):
-    for w in range(2):
-        crossed = owners_ref[w, 0] >= 64
-        block = jnp.where(crossed, other_ref[w].astype(F32), own_ref[w].astype(F32)).astype(BF)
-        out_ref[:, 8 * w : 8 * w + 8, :] = jnp.broadcast_to(block[None], (64, 8, L))
+    for dest in range(2):
+        w = jnp.where(owners_ref[0, dest] // 64 == row, 0, 1)
+        start = pl.multiple_of(8 + 8 * w, 8)
+        block = got_ref[owners_ref[w, dest] % 64, pl.ds(start, 8), :]
+        out_ref[64 * dest : 64 * dest + 64] = jnp.broadcast_to(block[None], (64, 8, L))
 
 
 def prepare_kernel(part_ref, k_ref, got_ref, rev_ref, h, sems):
@@ -96,7 +89,7 @@
 
 
 def correlate_kernel(
-    counts_ref, whole, rev_ref, out_ref, flat, y64, lx, ly, ra, rb, scr, obuf, sems
+    counts_ref, owners_ref, whole, rev_ref, out_ref, flat, y64, lx, ly, ra, rb, scr, obuf, sems
 ):
     me = lax.axis_index(TMPL)
     tri = iota((L, L), 0) >= iota((L, L), 1)
@@ -150,7 +143,8 @@
     build(0, ra)
     lane = iota((68, L), 1)
     for w in range(2):
-        flat[w] = whole[:, 8 * w : 8 * w + 8, :].astype(F32).reshape(512, L)
+        held = owners_ref[w, lax.axis_index("trial")] // 64
+        flat[w] = whole[pl.ds(64 * held, 64)].astype(F32).reshape(512, L)
         top, low = slice(w * L, (w + 1) * L), slice(256 + w * L, 256 + (w + 1) * L)
         for c in range(2):
             even = flat[w, pl.ds(264 + c, 68, stride=2), :]
@@ -199,30 +193,25 @@
     sent = pl.pallas_call(
         pack_kernel,
         out_shape=jax.ShapeDtypeStruct((64, 24, L), BF),
-        in_specs=[VMEM, VMEM, ANY, ANY],
+        in_specs=[ANY] * 4,
         out_specs=ANY,
-        scratch_shapes=[pltpu.VMEM((64, 24, L), BF), dma((5,))],
+        scratch_shapes=[
+            pltpu.VMEM((8, L), jnp.int32),
+            pltpu.VMEM((L, L), BF),
+            pltpu.VMEM((64, 24, L), BF),
+            dma((7,)),
+        ],
         name="pack",
     )(partners.reshape(8, L), k, x, y)
     got = lax.all_to_all(sent, TMPL, 0, 0, tiled=True)
-    own = pl.pallas_call(
-        extract_kernel,
-        out_shape=jax.ShapeDtypeStruct((2, 8, L), BF),
-        in_specs=[SMEM, ANY],
-        out_specs=VMEM,
-        scratch_shapes=[dma((2,))],
-        compiler_params=SMALL,
-        name="extract",
-    )(owners, got)
-    other = lax.ppermute(own, "trial", [(0, 1), (1, 0)])
     repeated = pl.pallas_call(
-        repeat_kernel,
-        out_shape=jax.ShapeDtypeStruct((64, 16, L), BF),
-        in_specs=[SMEM, VMEM, VMEM],
+        relay_kernel,
+        out_shape=jax.ShapeDtypeStruct((128, 8, L), BF),
+        in_specs=[SMEM, VMEM],
         out_specs=VMEM,
         compiler_params=SMALL,
-        name="repeat",
-    )(owners, own, other)
+        name="relay",
+    )(owners, got)
     rev = pl.pallas_call(
         prepare_kernel,
         out_shape=jax.ShapeDtypeStruct((2, L, L), F32),
@@ -233,11 +222,11 @@
         compiler_params=SMALL,
         name="prepare",
     )(partners, k, got)
-    whole = lax.all_to_all(repeated, TMPL, 0, 0, tiled=True)
+    whole = lax.all_to_all(repeated, ("trial",) + TMPL, 0, 0, tiled=True)
     out = pl.pallas_call(
         correlate_kernel,
         out_shape=jax.ShapeDtypeStruct((2, 16, 16384), BF),
-        in_specs=[SMEM, VMEM, VMEM],
+        in_specs=[SMEM, SMEM, VMEM, VMEM],
         out_specs=ANY,
         scratch_shapes=[
             pltpu.VMEM((2, 512, L), F32),
@@ -252,7 +241,7 @@
         ],
         compiler_params=LARGE,
         name="correlate",
-    )(counts, whole, rev)
+    )(counts, owners, whole, rev)
     return out[:, None]
 
 

time: 52.8 us -> 50.2 us (0.951)
  starting transfers between devices: 6.8 us -> 5.5 us
  Pallas kernels: 12.9 us -> 11.8 us
    ppermute x1 -> x0, starting transfers between devices: 2.04 us -> none  [body(): other = lax.ppermute(own, 'trial', [(0, 1), (1, 0)])]
    all_to_all x1, waiting for transfers between devices: 8.77 us -> 9.62 us  [body(): whole = lax.all_to_all(repeated, ('trial',) + TMPL, 0, 0, tiled=True)]
    ppermute x1 -> x0, waiting for transfers between devices: 0.82 us -> none  [body(): other = lax.ppermute(own, 'trial', [(0, 1), (1, 0)])]
    all_to_all x1, starting transfers between devices: 4.76 us -> 5.5 us  [body(): whole = lax.all_to_all(repeated, ('trial',) + TMPL, 0, 0, tiled=True)]
    pallas_call x2 -> x1, Pallas kernels: 1.9 us -> 1.31 us  [body(): pl.pallas_call(relay_kernel, out_shape=jax.ShapeDtypeStruct((128, 8, L),...]
    pallas_call x1, Pallas kernels: 2.51 us -> 1.96 us  [body(): pl.pallas_call(pack_kernel, out_shape=jax.ShapeDtypeStruct((64, 24, L), B...]
  transfers between devices with their start and end apart: 2 -> 1, of which waited for: 2 -> 1; matrix products, arithmetic and copies ran while one was open for 0% -> 0% of each run, Pallas kernels for 2% -> 2%
where the time goes in v5:
time: 50.2 us; the launch traced here: 49.8 us
  blocking collectives  22.9 us (46%)
  Pallas kernels  11.8 us (24%)
  waiting for transfers between devices  9.62 us (19%)
  starting transfers between devices  5.5 us (11%)
    all_to_all x1, blocking collectives, body(): got = lax.all_to_all(sent, TMPL, 0, 0, tiled=True)  22.9 us
    all_to_all x1, waiting for transfers between devices, body(): whole = lax.all_to_all(repeated, ('trial',) + TMPL, 0, 0, tiled=True)  9.62 us
    pallas_call x1, Pallas kernels, body(): pl.pallas_call(correlate_kernel, out_shape=jax.ShapeDtypeStruct((2, 16, 1...  7.32 us
    all_to_all x1, starting transfers between devices, body(): whole = lax.all_to_all(repeated, ('trial',) + TMPL, 0, 0, tiled=True)  5.5 us
    pallas_call x1, Pallas kernels, body(): pl.pallas_call(pack_kernel, out_shape=jax.ShapeDtypeStruct((64, 24, L), B...  1.96 us
    pallas_call x1, Pallas kernels, body(): pl.pallas_call(relay_kernel, out_shape=jax.ShapeDtypeStruct((128, 8, L),...  1.31 us
    pallas_call x1, Pallas kernels, body(): pl.pallas_call(prepare_kernel, out_shape=jax.ShapeDtypeStruct((2, L, L),...  1.17 us
  transfers between devices with their start and end apart: 1, of which 1 were waited for; matrix products, arithmetic and copies ran while one was open for 0% of the time, Pallas kernels for 2%

profile of v5, /device:TPU:1, one launch (start us, length us, event | category | flops | bytes accessed | tf_op | source)
XLA Modules:
  0.0 49.8 jit_solution(1795736374310407369)
XLA Ops:
  0.0 2.0 %pack.1 = bf16[64,24,128]{2,1,0:T(8,128)(2,1)} custom-call(s32[8,128]{1,0:T(8,128)} %bitcast.21, bf16[128,128]{1,0:T(8,128)(2,1)} %bitcast.19, bf16[2,33,8,128]{3,2,1,0:T(8,128)(2,1)} %bitcast.22, bf16[2,17,8,128]{3,2,1,0:T(8,128)(2,1)} %bitcast.23), custom_call_target="tpu_custom_call" | custom-call | tf_op jit(solution)/shard_map/pack/pallas_call | solution.py:193
  2.0 0.0 copy-start.2
  2.0 22.9 %all_to_all.10.got_ref = bf16[64,24,128]{2,1,0:T(8,128)(2,1)S(1)} all-to-all(bf16[64,24,128]{2,1,0:T(8,128)(2,1)} %pack.1), channel_id=1, replica_groups=mesh['trial'=2,'tmpl_0'=4,'tmpl_1'=4,'tmpl_2'=4] {'tmpl_0','tmpl_1','tmp..., dimensions={0} | all-to-all | bytes 786432 | tf_op jit(solution)/shard_map/all_to_all | solution.py:206
  24.9 0.0 copy-done.2
  24.9 1.3 %relay.1 = bf16[128,8,128]{2,1,0:T(8,128)(2,1)} custom-call(s32[2,2]{1,0:T(2,128)S(1)} %copy-done.2, bf16[64,24,128]{2,1,0:T(8,128)(2,1)S(1)} %all_to_all.10.got_ref), custom_call_target="tpu_custom_call" | custom-call | tf_op jit(solution)/shard_map/relay/pallas_call | solution.py:207
  26.2 0.0 copy-start
  26.2 0.0 copy-start.1
  26.2 5.5 %all-to-all-start.1 = ((bf16[128,8,128]{2,1,0:T(8,128)(2,1)}), bf16[128,8,128]{2,1,0:T(8,128)(2,1)S(1)}, u32[]{:S(2)}, u32[]{:S(2)}) async-start(bf16[128,8,128]{2,1,0:T(8,128)(2,1)} %relay.1), calls=%async_computation.1 | async-start | bytes 524288 | tf_op jit(solution)/shard_map/all_to_all | solution.py:225
  31.7 0.0 copy-done
  31.7 0.0 copy-done.1
  31.7 0.0 copy-start.3
  31.7 1.2 %prepare.1.rev_ref = f32[2,128,128]{2,1,0:T(8,128)S(1)} custom-call(s32[1024]{0:T(1024)S(1)} %copy-done.1, bf16[128,128]{1,0:T(8,128)(2,1)S(1)} %bitcast.20, bf16[64,24,128]{2,1,0:T(8,128)(2,1)S(1)} %all_to_all.10.got_ref), custom_call_target="tpu_custom_call" | custom-call | flops 10000000 | bytes 1000000 | tf_op jit(solution)/shard_map/prepare/pallas_call | solution.py:215
  32.9 9.6 %all-to-all-done.1.whole = bf16[128,8,128]{2,1,0:T(8,128)(2,1)S(1)} async-done(((bf16[128,8,128]{2,1,0:T(8,128)(2,1)}), bf16[128,8,128]{2,1,0:T(8,128)(2,1)S(1)}, u32[]{:S(2)}, u32[]{:S(2)}) %all-to-all-start.1) | async-done | bytes 262176 | tf_op jit(solution)/shard_map/all_to_all | solution.py:225
  42.5 0.0 copy-done.3
  42.5 7.3 %correlate.1 = bf16[2,16,16384]{2,1,0:T(8,128)(2,1)} custom-call(s32[64]{0:T(128)S(1)} %copy-done.3, s32[2,2]{1,0:T(2,128)S(1)} %copy-done.2, bf16[128,8,128]{2,1,0:T(8,128)(2,1)S(1)} %all-to-all-done.1.whole, f32[2,128,128]{2,1,0:T(8,128)S(1)} %prepare.1.rev_ref), custom_call_target="tpu_custom_call" | custom-call | tf_op jit(solution)/shard_map/correlate/pallas_call | solution.py:226
Async XLA Ops:
  2.0 22.9 %copy-start.2 = (s32[2,2]{1,0:T(2,128)S(1)}, s32[2,2]{1,0:T(2,128)}, u32[]{:S(2)}) copy-start(s32[2,2]{1,0:T(2,128)} %owners_ref.3) | copy-start | bytes 52
  26.2 5.5 %copy-start = (bf16[16,2,512]{2,1,0:T(2,128)(2,1)S(1)}, bf16[16,2,512]{2,1,0:T(2,128)(2,1)}, u32[]{:S(2)}) copy-start(bf16[16,2,512]{2,1,0:T(2,128)(2,1)} %param.8) | copy-start | bytes 98308
  26.2 5.5 %copy-start.1 = (s32[1024]{0:T(1024)S(1)}, s32[1024]{0:T(1024)}, u32[]{:S(2)}) copy-start(s32[1024]{0:T(1024)} %part_ref.1) | copy-start | bytes 12292
  26.2 16.3 %all-to-all-start.1 = ((bf16[128,8,128]{2,1,0:T(8,128)(2,1)}), bf16[128,8,128]{2,1,0:T(8,128)(2,1)S(1)}, u32[]{:S(2)}, u32[]{:S(2)}) async-start(bf16[128,8,128]{2,1,0:T(8,128)(2,1)} %relay.1), calls=%async_computation.1 | async-start | bytes 524288 | tf_op jit(solution)/shard_map/all_to_all | solution.py:225
  31.7 10.8 %copy-start.3 = (s32[64]{0:T(128)S(1)}, s32[64]{0:T(128)}, u32[]{:S(2)}) copy-start(s32[64]{0:T(128)} %counts_ref.1) | copy-start | bytes 772

commit v6 on v5

v6 whole, which is shorter than its diff:
```python
import jax
import jax.numpy as jnp
from jax import lax
from jax.experimental import pallas as pl
from jax.experimental.pallas import tpu as pltpu
from jax.sharding import Mesh
from jax.sharding import PartitionSpec as P

TMPL = ("tmpl_0", "tmpl_1", "tmpl_2")
F32 = jnp.float32
BF = jnp.bfloat16
L = 128
VMEM = pl.BlockSpec(memory_space=pltpu.VMEM)
SMEM = pl.BlockSpec(memory_space=pltpu.SMEM)
ANY = pl.BlockSpec(memory_space=pl.ANY)
SMALL = pltpu.CompilerParams(vmem_limit_bytes=4 << 20)
LARGE = pltpu.CompilerParams(vmem_limit_bytes=24 << 20)


def iota(shape, axis):
    return lax.broadcasted_iota(jnp.int32, shape, axis)


def dot(a, b):
    return jnp.dot(a, b, preferred_element_type=F32)


def pack_kernel(part_hbm, k_hbm, x_ref, y_ref, buf, part_ref, k_ref, sems):
    me = lax.axis_index(TMPL)
    tables = (
        pltpu.make_async_copy(part_hbm, part_ref, sems.at[4]),
        pltpu.make_async_copy(k_hbm, k_ref, sems.at[5]),
    )
    for table in tables:
        table.start()
    loads = []
    for w in range(2):
        rows = slice(8 + 8 * w, 16 + 8 * w)
        loads.append(pltpu.make_async_copy(x_ref.at[w], buf.at[0:33, rows, :], sems.at[2 * w]))
        loads.append(pltpu.make_async_copy(y_ref.at[w], buf.at[33:50, rows, :], sems.at[2 * w + 1]))
    for load in loads:
        load.start()
    buf[50:64, 8:24, :] = jnp.zeros((14, 16, L), BF)
    group = (iota((64, L), 0) // 8 == iota((64, L), 1) // 16).astype(BF)
    same = iota((64, L), 0) % 8 == iota((64, L), 1) % 8
    for table in tables:
        table.wait()
    wanted = jnp.concatenate(
        [
            (jnp.broadcast_to(part_ref[r : r + 1, :], (L, L)) == me * 16 + iota((L, L), 0) // 8).astype(BF)
            for r in range(8)
        ],
        axis=0,
    )
    hit = lax.dot_general(group, wanted, (((1,), (1,)), ((), ())), preferred_element_type=F32)
    pick = jnp.concatenate(
        [jnp.where(same, hit[:, r * L : (r + 1) * L], 0.0).astype(BF) for r in range(8)], axis=0
    )
    buf[:, 0:8, :] = dot(pick, k_ref[...]).reshape(64, 8, L).astype(BF)
    for load in loads:
        load.wait()


def relay_kernel(owners_ref, got_ref, out_ref):
    row = lax.axis_index("trial")
    for dest in range(2):
        w = jnp.where(owners_ref[0, dest] // 64 == row, 0, 1)
        start = pl.multiple_of(8 + 8 * w, 8)
        block = got_ref[owners_ref[w, dest] % 64, pl.ds(start, 8), :]
        out_ref[64 * dest : 64 * dest + 64] = jnp.broadcast_to(block[None], (64, 8, L))


class Taps:
    def __init__(self, rev_ref):
        self.rev = rev_ref
        self.tri = iota((L, L), 0) >= iota((L, L), 1)
        self.tri_half = iota((L, L), 0) >= iota((L, L), 1) % 64
        self.left = iota((L, L), 1) < 64
        self.zero = jnp.zeros((L, L), F32)

    def circulant(self, kind, row, shift):
        v = jnp.broadcast_to(self.rev[kind, pl.ds(row, 1), :], (L, L))
        return pltpu.roll(v, shift, 1, stride=1, stride_axis=0)

    def put(self, dst, c, side, cs, mask):
        lower = cs + [self.zero]
        upper = [self.zero] + cs
        for q in range(5):
            tile = jnp.where(mask, lower[q], upper[q]).astype(BF)
            dst[(5 * c + q) * L : (5 * c + q + 1) * L, side * L : (side + 1) * L] = tile

    def direct(self, pair, dst):
        for k in range(2):
            for c in range(2):
                row = (2 * pair + k) * 8 + c
                self.put(dst, c, k, [self.circulant(0, row + 2 * q, 0) for q in range(4)], self.tri)

    def plane(self, group, dst):
        for k in range(2):
            for c in range(2):
                row = (4 * group + 2 * k) * 8 + c
                both = [
                    jnp.where(self.left, self.circulant(1, row + 2 * q, 0), self.circulant(1, row + 8 + 2 * q, 64))
                    for q in range(4)
                ]
                self.put(dst, c, k, both, self.tri_half)


def prepare_kernel(part_ref, k_ref, got_ref, rev_ref, ahead_ref, h, sems):
    me = lax.axis_index(TMPL)
    copies = []
    for s in range(16):
        source = jnp.maximum(part_ref[me * 16 + s], 0) // 16
        copies.append(pltpu.make_async_copy(got_ref.at[source, 0:8, :], h.at[s], sems.at[s]))
    for copy in copies:
        copy.start()
    flip = (iota((L, L), 0) == (L - iota((L, L), 1)) % L).astype(BF)
    rev_ref[0] = dot(k_ref[...], flip)
    for copy in copies:
        copy.wait()
    rev_ref[1] = dot(h[...].astype(F32).reshape(L, L).astype(BF), flip)
    taps = Taps(rev_ref)
    for group in range(2):
        taps.plane(group, ahead_ref.at[group])


def correlate_kernel(
    counts_ref, owners_ref, whole, rev_ref, ahead, out_ref, flat, y64, lx, ly, rp, rd, scr, obuf, sems
):
    me = lax.axis_index(TMPL)
    live_n = counts_ref[me]
    taps = Taps(rev_ref)

    dup = (iota((L, 2 * L), 0) == (iota((L, 2 * L), 1) // L) * 64 + (iota((L, 2 * L), 1) % L) // 2).astype(BF)

    def power(rows, w, operand):
        z = dot(rows[256 * w : 256 * w + 256, :], operand[...])
        return z[:L] * z[:L] + z[L:] * z[L:]

    def finish(pair, w, plane):
        wide = dot(plane[:, (pair % 2) * L : (pair % 2 + 1) * L], dup)
        total = power(lx, w, rd.at[pair]) + wide
        for j in range(2):
            t = 2 * pair + j
            rows = pl.ds(w * 2048 + t, L, stride=16)
            scr[rows, :] = jnp.where(t < live_n, total[:, j * L : (j + 1) * L], 0.0)

    stores = []

    def merge(w):
        for part in range(4):
            for a in range(32 * part, 32 * part + 32):
                rows = slice((w * L + a) * 16, (w * L + a + 1) * 16)
                obuf[w, :, a * L : (a + 1) * L] = scr[rows, :].astype(BF)
            cols = slice(part * 4096, (part + 1) * 4096)
            copy = pltpu.make_async_copy(obuf.at[w, :, cols], out_ref.at[w, :, cols], sems.at[4 * w + part])
            copy.start()
            stores.append(copy)

    lane = iota((68, L), 1)
    for w in range(2):
        held = owners_ref[w, lax.axis_index("trial")] // 64
        flat[w] = whole[pl.ds(64 * held, 64)].astype(F32).reshape(512, L)
        top, low = slice(256 * w, 256 * w + L), slice(256 * w + L, 256 * w + 256)
        for c in range(2):
            even = flat[w, pl.ds(264 + c, 68, stride=2), :]
            after = flat[w, pl.ds(266 + c, 68, stride=2), :]
            y64[pl.ds(0, 68, stride=2), :] = even
            y64[pl.ds(1, 68, stride=2), :] = jnp.where(lane < 64, pltpu.roll(even, 64, 1), pltpu.roll(after, 64, 1))
            for q in range(5):
                here = slice((5 * c + q) * L, (5 * c + q + 1) * L)
                there = slice((5 - 5 * c + q) * L, (6 - 5 * c + q) * L)
                for dst, v in (
                    (lx, flat[w, pl.ds(2 * q + c, L, stride=2), :]),
                    (ly, y64[2 * q : 2 * q + L, :]),
                ):
                    dst[top, here] = (v if c == 0 else -v).astype(BF)
                    dst[low, there] = v.astype(BF)

    for half in range(2):
        pairs = range(4 * half, 4 * half + 4)
        taps.direct(pairs[0], rd.at[pairs[0]])
        taps.direct(pairs[1], rd.at[pairs[1]])
        planes = [[power(ly, w, (rp if half else ahead).at[k]).astype(BF) for w in range(2)] for k in range(2)]
        taps.direct(pairs[2], rd.at[pairs[2]])
        taps.direct(pairs[3], rd.at[pairs[3]])
        if half == 0:
            for pair in pairs:
                if pair == 2:
                    taps.plane(2, rp.at[0])
                    taps.plane(3, rp.at[1])
                for w in range(2):
                    finish(pair, w, planes[pair // 2 % 2][w])
        else:
            for w in range(2):
                for pair in pairs:
                    finish(pair, w, planes[pair // 2 % 2][w])
                merge(w)
    for store in stores:
        store.wait()


def body(spectra, half_spectra, kernels, owners, counts, partners):
    x = spectra.reshape(2, 2, 33, 4, L).transpose(0, 2, 3, 1, 4).reshape(2, 33, 8, L)
    y = half_spectra.reshape(2, 2, 17, 4, L).transpose(0, 2, 3, 1, 4).reshape(2, 17, 8, L)
    k = kernels.reshape(16, 2, 4, L).transpose(0, 2, 1, 3).reshape(L, L)
    dma = pltpu.SemaphoreType.DMA
    sent = pl.pallas_call(
        pack_kernel,
        out_shape=jax.ShapeDtypeStruct((64, 24, L), BF),
        in_specs=[ANY] * 4,
        out_specs=VMEM,
        scratch_shapes=[pltpu.VMEM((8, L), jnp.int32), pltpu.VMEM((L, L), BF), dma((6,))],
        compiler_params=pltpu.CompilerParams(vmem_limit_bytes=4194304),
        name="pack",
    )(*[pltpu.with_memory_space_constraint(v, pltpu.HBM) for v in (partners.reshape(8, L), k, x, y)])
    got = lax.all_to_all(sent, TMPL, 0, 0, tiled=True)
    repeated = pl.pallas_call(
        relay_kernel,
        out_shape=jax.ShapeDtypeStruct((128, 8, L), BF),
        in_specs=[SMEM, VMEM],
        out_specs=VMEM,
        compiler_params=SMALL,
        name="relay",
    )(owners, got)
    rev, ahead = pl.pallas_call(
        prepare_kernel,
        out_shape=(
            jax.ShapeDtypeStruct((2, L, L), F32),
            jax.ShapeDtypeStruct((2, 1280, 256), BF),
        ),
        in_specs=[SMEM, VMEM, ANY],
        out_specs=(VMEM, VMEM),
        scratch_shapes=[pltpu.VMEM((16, 8, L), BF), dma((16,))],
        cost_estimate=pl.CostEstimate(flops=10**7, bytes_accessed=10**6, transcendentals=0),
        compiler_params=SMALL,
        name="prepare",
    )(partners, k, got)
    whole = lax.all_to_all(repeated, ("trial",) + TMPL, 0, 0, tiled=True)
    out = pl.pallas_call(
        correlate_kernel,
        out_shape=jax.ShapeDtypeStruct((2, 16, 16384), BF),
        in_specs=[SMEM, SMEM, VMEM, VMEM, VMEM],
        out_specs=ANY,
        scratch_shapes=[
            pltpu.VMEM((2, 512, L), F32),
            pltpu.VMEM((136, L), F32),
            pltpu.VMEM((512, 1280), BF),
            pltpu.VMEM((512, 1280), BF),
            pltpu.VMEM((2, 1280, 256), BF),
            pltpu.VMEM((8, 1280, 256), BF),
            pltpu.VMEM((4096, L), F32),
            pltpu.VMEM((2, 16, 16384), BF),
            dma((8,)),
        ],
        compiler_params=LARGE,
        name="correlate",
    )(counts, owners, whole, rev, ahead)
    return out[:, None]


def solution(mesh):
    finer = Mesh(
        mesh.devices.reshape(mesh.shape["trial"], 4, 4, 4), ("trial", "tmpl_0", "tmpl_1", "tmpl_2")
    )
    in_specs = (
        P(None, "trial", TMPL, None, None),
        P(None, "trial", TMPL, None, None),
        P(TMPL, None, None),
        P(),
        P(),
        P(),
    )
    out_specs = P(None, "trial", TMPL, None)
    return jax.shard_map(body, mesh=finer, in_specs=in_specs, out_specs=out_specs, check_vma=False)
```

time: 50.2 us -> 48.7 us (0.970)
  waiting for transfers between devices: 9.62 us -> 9 us
    pallas_call x1, Pallas kernels: 1.96 us -> 1.26 us  [body(): pl.pallas_call(pack_kernel, out_shape=jax.ShapeDtypeStruct((64, 24, L), B...]
    all_to_all x1, waiting for transfers between devices: 9.62 us -> 9 us  [body(): whole = lax.all_to_all(repeated, ('trial',) + TMPL, 0, 0, tiled=True)]
    pallas_call x1, Pallas kernels: 1.17 us -> 1.77 us  [body(): pl.pallas_call(prepare_kernel, out_shape=(jax.ShapeDtypeStruct((2, L, L),...]
  transfers between devices with their start and end apart: 1 -> 1, of which waited for: 1 -> 1; matrix products, arithmetic and copies ran while one was open for 0% -> 0% of each run, Pallas kernels for 2% -> 4%
where the time goes in v6:
time: 48.7 us; the launch traced here: 48.5 us
  blocking collectives  22.7 us (47%)
  Pallas kernels  11.3 us (23%)
  waiting for transfers between devices  9 us (18%)
  starting transfers between devices  5.4 us (11%)
    all_to_all x1, blocking collectives, body(): got = lax.all_to_all(sent, TMPL, 0, 0, tiled=True)  22.7 us
    all_to_all x1, waiting for transfers between devices, body(): whole = lax.all_to_all(repeated, ('trial',) + TMPL, 0, 0, tiled=True)  9 us
    pallas_call x1, Pallas kernels, body(): pl.pallas_call(correlate_kernel, out_shape=jax.ShapeDtypeStruct((2, 16, 1...  6.97 us
    all_to_all x1, starting transfers between devices, body(): whole = lax.all_to_all(repeated, ('trial',) + TMPL, 0, 0, tiled=True)  5.4 us
    pallas_call x1, Pallas kernels, body(): pl.pallas_call(prepare_kernel, out_shape=(jax.ShapeDtypeStruct((2, L, L),...  1.77 us
    pallas_call x1, Pallas kernels, body(): pl.pallas_call(relay_kernel, out_shape=jax.ShapeDtypeStruct((128, 8, L),...  1.31 us
    pallas_call x1, Pallas kernels, body(): pl.pallas_call(pack_kernel, out_shape=jax.ShapeDtypeStruct((64, 24, L), B...  1.26 us
  transfers between devices with their start and end apart: 1, of which 1 were waited for; matrix products, arithmetic and copies ran while one was open for 0% of the time, Pallas kernels for 4%

profile of v6, /device:TPU:1, one launch (start us, length us, event | category | flops | bytes accessed | tf_op | source)
XLA Modules:
  0.0 48.5 jit_solution(3663806578249036486)
XLA Ops:
  0.0 0.0 copy-start.1
  0.0 0.0 copy-start
  0.0 0.0 copy-start.2
  0.0 1.3 %pack.1 = bf16[64,24,128]{2,1,0:T(8,128)(2,1)S(1)} custom-call(s32[8,128]{1,0:T(8,128)} %bitcast.21, bf16[128,128]{1,0:T(8,128)(2,1)} %bitcast.19, bf16[2,33,8,128]{3,2,1,0:T(8,128)(2,1)} %bitcast.22, bf16[2,17,8,128]{3,2,1,0:T(8,128)(2,1)} %bitcast.23), custom_call_target="tpu_custom_call" | custom-call | tf_op jit(solution)/shard_map/pack/pallas_call | solution.py:208
  1.3 0.0 copy-start.3
  1.3 22.7 %all_to_all.10.got_ref = bf16[64,24,128]{2,1,0:T(8,128)(2,1)S(1)} all-to-all(bf16[64,24,128]{2,1,0:T(8,128)(2,1)S(1)} %pack.1), channel_id=1, replica_groups=mesh['trial'=2,'tmpl_0'=4,'tmpl_1'=4,'tmpl_2'=4] {'tmpl_0','tmpl_1','tmp..., dimensions={0} | all-to-all | bytes 786432 | tf_op jit(solution)/shard_map/all_to_all | solution.py:217
  24.0 0.0 copy-done.2
  24.0 1.3 %relay.1 = bf16[128,8,128]{2,1,0:T(8,128)(2,1)} custom-call(s32[2,2]{1,0:T(2,128)S(1)} %copy-done.2, bf16[64,24,128]{2,1,0:T(8,128)(2,1)S(1)} %all_to_all.10.got_ref), custom_call_target="tpu_custom_call" | custom-call | tf_op jit(solution)/shard_map/relay/pallas_call | solution.py:218
  25.3 5.4 %all-to-all-start.1 = ((bf16[128,8,128]{2,1,0:T(8,128)(2,1)}), bf16[128,8,128]{2,1,0:T(8,128)(2,1)S(1)}, u32[]{:S(2)}, u32[]{:S(2)}) async-start(bf16[128,8,128]{2,1,0:T(8,128)(2,1)} %relay.1), calls=%async_computation.1 | async-start | bytes 524288 | tf_op jit(solution)/shard_map/all_to_all | solution.py:239
  30.7 0.0 copy-done.1
  30.7 0.0 copy-done
  30.7 1.8 %prepare.1 = (f32[2,128,128]{2,1,0:T(8,128)S(1)}, bf16[2,1280,256]{2,1,0:T(8,128)(2,1)S(1)}) custom-call(s32[1024]{0:T(1024)S(1)} %copy-done.1, bf16[128,128]{1,0:T(8,128)(2,1)S(1)} %bitcast.20, bf16[64,24,128]{2,1,0:T(8,128)(2,1)S(1)} %all_to_all.10.got_ref), custom_call_target="tpu_custom_call" | custom-call | flops 10000000 | bytes 1000000 | tf_op jit(solution)/shard_map/prepare/pallas_call | solution.py:226
  32.5 9.0 %all-to-all-done.1.whole = bf16[128,8,128]{2,1,0:T(8,128)(2,1)S(1)} async-done(((bf16[128,8,128]{2,1,0:T(8,128)(2,1)}), bf16[128,8,128]{2,1,0:T(8,128)(2,1)S(1)}, u32[]{:S(2)}, u32[]{:S(2)}) %all-to-all-start.1) | async-done | bytes 262176 | tf_op jit(solution)/shard_map/all_to_all | solution.py:239
  41.5 0.0 copy-done.3
  41.5 7.0 %correlate.1 = bf16[2,16,16384]{2,1,0:T(8,128)(2,1)} custom-call(s32[64]{0:T(128)S(1)} %copy-done.3, s32[2,2]{1,0:T(2,128)S(1)} %copy-done.2, bf16[128,8,128]{2,1,0:T(8,128)(2,1)S(1)} %all-to-all-done.1.whole, f32[2,128,128]{2,1,0:T(8,128)S(1)} %get-tuple-element.7.rev_ref, bf16[2,1280,256]{2,1,0:T(8,128)(2,1)S(1)} %get-tuple-element.8.ahead), custom_call_target="tpu_custom_call" | custom-call | tf_op jit(solution)/shard_map/correlate/pallas_call | solution.py:240
Async XLA Ops:
  0.0 30.7 %copy-start.1 = (s32[1024]{0:T(1024)S(1)}, s32[1024]{0:T(1024)}, u32[]{:S(2)}) copy-start(s32[1024]{0:T(1024)} %part_ref.1) | copy-start | bytes 12292
  0.0 30.7 %copy-start = (bf16[16,2,512]{2,1,0:T(2,128)(2,1)S(1)}, bf16[16,2,512]{2,1,0:T(2,128)(2,1)}, u32[]{:S(2)}) copy-start(bf16[16,2,512]{2,1,0:T(2,128)(2,1)} %param.8) | copy-start | bytes 98308
  0.0 23.9 %copy-start.2 = (s32[2,2]{1,0:T(2,128)S(1)}, s32[2,2]{1,0:T(2,128)}, u32[]{:S(2)}) copy-start(s32[2,2]{1,0:T(2,128)} %owners_ref.3) | copy-start | bytes 52
  1.3 40.2 %copy-start.3 = (s32[64]{0:T(128)S(1)}, s32[64]{0:T(128)}, u32[]{:S(2)}) copy-start(s32[64]{0:T(128)} %counts_ref.1) | copy-start | bytes 772
  25.3 16.2 %all-to-all-start.1 = ((bf16[128,8,128]{2,1,0:T(8,128)(2,1)}), bf16[128,8,128]{2,1,0:T(8,128)(2,1)S(1)}, u32[]{:S(2)}, u32[]{:S(2)}) async-start(bf16[128,8,128]{2,1,0:T(8,128)(2,1)} %relay.1), calls=%async_computation.1 | async-start | bytes 524288 | tf_op jit(solution)/shard_map/all_to_all | solution.py:239

commit v7 on v6

--- a/solution.py
+++ b/solution.py
@@ -25,7 +25,7 @@
     return jnp.dot(a, b, preferred_element_type=F32)
 
 
-def pack_kernel(part_hbm, k_hbm, x_ref, y_ref, buf, part_ref, k_ref, sems):
+def pack_kernel(part_hbm, k_hbm, x_ref, y_ref, buf, rev_ref, part_ref, k_ref, sems):
     me = lax.axis_index(TMPL)
     tables = (
         pltpu.make_async_copy(part_hbm, part_ref, sems.at[4]),
@@ -52,22 +52,30 @@
         ],
         axis=0,
     )
+    flip = (iota((L, L), 0) == (L - iota((L, L), 1)) % L).astype(BF)
+    rev = dot(k_ref[...], flip).astype(BF)
+    rev_ref[...] = rev
     hit = lax.dot_general(group, wanted, (((1,), (1,)), ((), ())), preferred_element_type=F32)
     pick = jnp.concatenate(
         [jnp.where(same, hit[:, r * L : (r + 1) * L], 0.0).astype(BF) for r in range(8)], axis=0
     )
-    buf[:, 0:8, :] = dot(pick, k_ref[...]).reshape(64, 8, L).astype(BF)
+    buf[:, 0:8, :] = dot(pick, rev).reshape(64, 8, L).astype(BF)
     for load in loads:
         load.wait()
 
 
-def relay_kernel(owners_ref, got_ref, out_ref):
+def relay_kernel(owners_ref, part_ref, own_ref, got_ref, out_ref, rev_ref):
+    me = lax.axis_index(TMPL)
     row = lax.axis_index("trial")
     for dest in range(2):
         w = jnp.where(owners_ref[0, dest] // 64 == row, 0, 1)
         start = pl.multiple_of(8 + 8 * w, 8)
         block = got_ref[owners_ref[w, dest] % 64, pl.ds(start, 8), :]
         out_ref[64 * dest : 64 * dest + 64] = jnp.broadcast_to(block[None], (64, 8, L))
+    rev_ref[0] = own_ref[...].astype(F32)
+    for s in range(16):
+        source = jnp.maximum(part_ref[me * 16 + s], 0) // 16
+        rev_ref[1, 8 * s : 8 * s + 8, :] = got_ref[source, 0:8, :].astype(F32)
 
 
 class Taps:
@@ -106,26 +114,8 @@
                 self.put(dst, c, k, both, self.tri_half)
 
 
-def prepare_kernel(part_ref, k_ref, got_ref, rev_ref, ahead_ref, h, sems):
-    me = lax.axis_index(TMPL)
-    copies = []
-    for s in range(16):
-        source = jnp.maximum(part_ref[me * 16 + s], 0) // 16
-        copies.append(pltpu.make_async_copy(got_ref.at[source, 0:8, :], h.at[s], sems.at[s]))
-    for copy in copies:
-        copy.start()
-    flip = (iota((L, L), 0) == (L - iota((L, L), 1)) % L).astype(BF)
-    rev_ref[0] = dot(k_ref[...], flip)
-    for copy in copies:
-        copy.wait()
-    rev_ref[1] = dot(h[...].astype(F32).reshape(L, L).astype(BF), flip)
-    taps = Taps(rev_ref)
-    for group in range(2):
-        taps.plane(group, ahead_ref.at[group])
-
-
 def correlate_kernel(
-    counts_ref, owners_ref, whole, rev_ref, ahead, out_ref, flat, y64, lx, ly, rp, rd, scr, obuf, sems
+    counts_ref, owners_ref, whole, rev_ref, out_ref, flat, y64, lx, ly, rp, rd, scr, obuf, sems
 ):
     me = lax.axis_index(TMPL)
     live_n = counts_ref[me]
@@ -157,6 +147,8 @@
             copy.start()
             stores.append(copy)
 
+    taps.plane(0, rp.at[0])
+    taps.plane(1, rp.at[1])
     lane = iota((68, L), 1)
     for w in range(2):
         held = owners_ref[w, lax.axis_index("trial")] // 64
@@ -181,14 +173,14 @@
         pairs = range(4 * half, 4 * half + 4)
         taps.direct(pairs[0], rd.at[pairs[0]])
         taps.direct(pairs[1], rd.at[pairs[1]])
-        planes = [[power(ly, w, (rp if half else ahead).at[k]).astype(BF) for w in range(2)] for k in range(2)]
+        planes = [[power(ly, w, rp.at[2 * half + k]).astype(BF) for w in range(2)] for k in range(2)]
         taps.direct(pairs[2], rd.at[pairs[2]])
         taps.direct(pairs[3], rd.at[pairs[3]])
         if half == 0:
             for pair in pairs:
                 if pair == 2:
-                    taps.plane(2, rp.at[0])
-                    taps.plane(3, rp.at[1])
+                    taps.plane(2, rp.at[2])
+                    taps.plane(3, rp.at[3])
                 for w in range(2):
                     finish(pair, w, planes[pair // 2 % 2][w])
         else:
@@ -205,49 +197,36 @@
     y = half_spectra.reshape(2, 2, 17, 4, L).transpose(0, 2, 3, 1, 4).reshape(2, 17, 8, L)
     k = kernels.reshape(16, 2, 4, L).transpose(0, 2, 1, 3).reshape(L, L)
     dma = pltpu.SemaphoreType.DMA
-    sent = pl.pallas_call(
+    sent, own = pl.pallas_call(
         pack_kernel,
-        out_shape=jax.ShapeDtypeStruct((64, 24, L), BF),
+        out_shape=(jax.ShapeDtypeStruct((64, 24, L), BF), jax.ShapeDtypeStruct((L, L), BF)),
         in_specs=[ANY] * 4,
-        out_specs=VMEM,
+        out_specs=(VMEM, VMEM),
         scratch_shapes=[pltpu.VMEM((8, L), jnp.int32), pltpu.VMEM((L, L), BF), dma((6,))],
         compiler_params=pltpu.CompilerParams(vmem_limit_bytes=4194304),
         name="pack",
     )(*[pltpu.with_memory_space_constraint(v, pltpu.HBM) for v in (partners.reshape(8, L), k, x, y)])
     got = lax.all_to_all(sent, TMPL, 0, 0, tiled=True)
-    repeated = pl.pallas_call(
+    repeated, rev = pl.pallas_call(
         relay_kernel,
-        out_shape=jax.ShapeDtypeStruct((128, 8, L), BF),
-        in_specs=[SMEM, VMEM],
-        out_specs=VMEM,
+        out_shape=(jax.ShapeDtypeStruct((128, 8, L), BF), jax.ShapeDtypeStruct((2, L, L), F32)),
+        in_specs=[SMEM, SMEM, VMEM, VMEM],
+        out_specs=(VMEM, VMEM),
         compiler_params=SMALL,
         name="relay",
-    )(owners, got)
-    rev, ahead = pl.pallas_call(
-        prepare_kernel,
-        out_shape=(
-            jax.ShapeDtypeStruct((2, L, L), F32),
-            jax.ShapeDtypeStruct((2, 1280, 256), BF),
-        ),
-        in_specs=[SMEM, VMEM, ANY],
-        out_specs=(VMEM, VMEM),
-        scratch_shapes=[pltpu.VMEM((16, 8, L), BF), dma((16,))],
-        cost_estimate=pl.CostEstimate(flops=10**7, bytes_accessed=10**6, transcendentals=0),
-        compiler_params=SMALL,
-        name="prepare",
-    )(partners, k, got)
+    )(*[pltpu.with_memory_space_constraint(v, pltpu.HBM) for v in (owners, partners)], own, got)
     whole = lax.all_to_all(repeated, ("trial",) + TMPL, 0, 0, tiled=True)
     out = pl.pallas_call(
         correlate_kernel,
         out_shape=jax.ShapeDtypeStruct((2, 16, 16384), BF),
-        in_specs=[SMEM, SMEM, VMEM, VMEM, VMEM],
+        in_specs=[SMEM, SMEM, VMEM, VMEM],
         out_specs=ANY,
         scratch_shapes=[
             pltpu.VMEM((2, 512, L), F32),
             pltpu.VMEM((136, L), F32),
             pltpu.VMEM((512, 1280), BF),
             pltpu.VMEM((512, 1280), BF),
-            pltpu.VMEM((2, 1280, 256), BF),
+            pltpu.VMEM((4, 1280, 256), BF),
             pltpu.VMEM((8, 1280, 256), BF),
             pltpu.VMEM((4096, L), F32),
             pltpu.VMEM((2, 16, 16384), BF),
@@ -255,7 +234,7 @@
         ],
         compiler_params=LARGE,
         name="correlate",
-    )(counts, owners, whole, rev, ahead)
+    )(*[pltpu.with_memory_space_constraint(v, pltpu.HBM) for v in (counts, owners)], whole, rev)
     return out[:, None]
 
 

time: 48.7 us -> 48.1 us (0.988)
  blocking collectives: 22.7 us -> 38.6 us
  waiting for transfers between devices: 9 us -> 0 us
  starting transfers between devices: 5.4 us -> 0 us
  Pallas kernels: 11.3 us -> 9.32 us
    all_to_all x0 -> x1, blocking collectives: none -> 15.9 us  [body(): whole = lax.all_to_all(repeated, ('trial',) + TMPL, 0, 0, tiled=True)]
    all_to_all x1 -> x0, waiting for transfers between devices: 9 us -> none  [body(): whole = lax.all_to_all(repeated, ('trial',) + TMPL, 0, 0, tiled=True)]
    all_to_all x1 -> x0, starting transfers between devices: 5.4 us -> none  [body(): whole = lax.all_to_all(repeated, ('trial',) + TMPL, 0, 0, tiled=True)]
    pallas_call x3 -> x2, Pallas kernels: 4.35 us -> 2.05 us  [the longest x1 1.2 us: body(): pl.pallas_call(pack_kernel, out_shape=(jax.ShapeDtypeStruct((64, 24, L),...]
  transfers between devices with their start and end apart: 1 -> 0, of which waited for: 1 -> 0; matrix products, arithmetic and copies ran while one was open for 0% -> 0% of each run, Pallas kernels for 4% -> 0%
where the time goes in v7:
time: 48.1 us; the launch traced here: 47.9 us
  blocking collectives  38.6 us (80%)
  Pallas kernels  9.32 us (19%)
    all_to_all x1, blocking collectives, body(): got = lax.all_to_all(sent, TMPL, 0, 0, tiled=True)  22.7 us
    all_to_all x1, blocking collectives, body(): whole = lax.all_to_all(repeated, ('trial',) + TMPL, 0, 0, tiled=True)  15.9 us
    pallas_call x1, Pallas kernels, body(): pl.pallas_call(correlate_kernel, out_shape=jax.ShapeDtypeStruct((2, 16, 1...  7.27 us
    pallas_call x1, Pallas kernels, body(): pl.pallas_call(pack_kernel, out_shape=(jax.ShapeDtypeStruct((64, 24, L),...  1.2 us

profile of v7, /device:TPU:1, one launch (start us, length us, event | category | flops | bytes accessed | tf_op | source)
XLA Modules:
  0.0 47.9 jit_solution(14517662540743482803)
XLA Ops:
  0.0 1.2 %pack.1 = (bf16[64,24,128]{2,1,0:T(8,128)(2,1)S(1)}, bf16[128,128]{1,0:T(8,128)(2,1)S(1)}) custom-call(s32[8,128]{1,0:T(8,128)} %bitcast.22, bf16[128,128]{1,0:T(8,128)(2,1)} %bitcast.21, bf16[2,33,8,128]{3,2,1,0:T(8,128)(2,1)} %bitcast.19, bf16[2,17,8,128]{3,2,1,0:T(8,128)(2,1)} %bitcast.20), custom_call_target="tpu_custom_call" | custom-call | tf_op jit(solution)/shard_map/pack/pallas_call | solution.py:200
  1.2 22.7 %all_to_all.10.got_ref = bf16[64,24,128]{2,1,0:T(8,128)(2,1)S(1)} all-to-all(bf16[64,24,128]{2,1,0:T(8,128)(2,1)S(1)} %get-tuple-element.10), channel_id=1, replica_groups=mesh['trial'=2,'tmpl_0'=4,'tmpl_1'=4,'tmpl_2'=4] {'tmpl_0','tmpl_1','tmp..., dimensions={0} | all-to-all | bytes 786432 | tf_op jit(solution)/shard_map/all_to_all | solution.py:209
  23.9 0.9 %relay.1 = (bf16[128,8,128]{2,1,0:T(8,128)(2,1)S(1)}, f32[2,128,128]{2,1,0:T(8,128)S(1)}) custom-call(s32[2,2]{1,0:T(2,128)} %owners_ref.3, s32[1024]{0:T(1024)} %part_ref.1, bf16[128,128]{1,0:T(8,128)(2,1)S(1)} %get-tuple-element.9.own_ref, bf16[64,24,128]{2,1,0:T(8,128)(2,1)S(1)} %all_to_all.10.got_ref), custom_call_target="tpu_custom_call" | custom-call | tf_op jit(solution)/shard_map/relay/pallas_call | solution.py:210
  24.7 15.9 %all_to_all.11.whole = bf16[128,8,128]{2,1,0:T(8,128)(2,1)S(1)} all-to-all(bf16[128,8,128]{2,1,0:T(8,128)(2,1)S(1)} %get-tuple-element.11), channel_id=1, replica_groups=mesh['trial'=2,'tmpl_0'=4,'tmpl_1'=4,'tmpl_2'=4] {'trial','tmpl_0','tmpl..., dimensions={0} | all-to-all | bytes 524288 | tf_op jit(solution)/shard_map/all_to_all | solution.py:218
  40.6 7.3 %correlate.1 = bf16[2,16,16384]{2,1,0:T(8,128)(2,1)} custom-call(s32[64]{0:T(128)} %counts_ref.1, s32[2,2]{1,0:T(2,128)} %owners_ref.3, bf16[128,8,128]{2,1,0:T(8,128)(2,1)S(1)} %all_to_all.11.whole, f32[2,128,128]{2,1,0:T(8,128)S(1)} %get-tuple-element.12.rev_ref), custom_call_target="tpu_custom_call" | custom-call | tf_op jit(solution)/shard_map/correlate/pallas_call | solution.py:219
